TPU v7x, 32 devices: a whole 2x2x4 slice. The times are simulated.
32 devices in a mesh: grp: 2 (over y), seq: 4 (over z), head: 2 (over x), sub: 2 (over core).
Axes of the slice: x: 2, y: 2, z: 4, core: 2. Of those that a mesh axis runs over, the one named last changes fastest.
Arguments:
- queries: bfloat16 [768, 5120], P(('grp', 'seq', 'head', 'sub')), parts along dimension 0, may hold values from -24 to 24
- keys: bfloat16 [768, 5120], P(('grp', 'seq', 'head', 'sub')), parts along dimension 0, may hold values from -24 to 24
- values: bfloat16 [768, 5120], P(('grp', 'seq', 'head', 'sub')), parts along dimension 0, may hold values from -6 to 6
- q_gain: float32 [5120], replicated, may hold values from 0.5 to 4
- k_gain: float32 [5120], replicated, may hold values from 0.5 to 4
Outputs:
- attended: bfloat16 [768, 5120], P(('grp', 'seq', 'head', 'sub')), parts along dimension 0
There are 2 independent parts, one for each index of `grp`. A program takes and returns all parts, laid end to end along the dimension named above; an argument that names none is the same for every part. Nothing has to cross between parts.
All inputs are finite; a program needn't handle non-finite values.
Results may differ from a plain program's by a relative error of at most 0.012.
The roundings to bfloat16 on the way count: a program that leaves them out, or rounds other values in their place, can miss the bound.
Values may be sent and summed in bfloat16 or wider, within the bound.
No kernel may reach another device: no remote copies, remote signals or barrier semaphores. Data moves between devices by JAX's collectives and lax.ppermute only.
A program may use at most 64 MiB of HBM per device.

v0:
```python
import math

import jax
import jax.numpy as jnp
from jax import lax
from jax.sharding import PartitionSpec as P

HD = 128


EPS = 1e-06


def normalize(matrix, gain):
    widened = matrix.astype(jnp.float32)
    inverse = lax.rsqrt(jnp.mean(widened * widened, axis=-1, keepdims=True) + EPS)
    return (widened * inverse * gain).astype(jnp.bfloat16)


def body(queries, keys, values, q_gain, k_gain):
    q_normed = normalize(queries, q_gain)
    k_normed = normalize(keys, k_gain)
    q_local, k_local, v_local = (
        lax.all_to_all(q_normed, "head", split_axis=1, concat_axis=0, tiled=True),
        lax.all_to_all(k_normed, "head", split_axis=1, concat_axis=0, tiled=True),
        lax.all_to_all(values, "head", split_axis=1, concat_axis=0, tiled=True),
    )
    query_count = q_local.shape[0]
    local_heads = q_local.shape[1] // HD
    factor = 1.0 / math.sqrt(HD)
    q_heads = q_local.reshape(query_count, local_heads, HD).transpose(1, 0, 2)
    initial = (
        jnp.full((local_heads, query_count), -1e30, jnp.float32),
        jnp.zeros((local_heads, query_count), jnp.float32),
        jnp.zeros((local_heads, query_count, HD), jnp.float32),
    )
    half_rows = q_local.shape[0]
    key_piece = lax.all_gather(k_local, ("seq", "sub"), axis=0, tiled=True)
    value_piece = lax.all_gather(v_local, ("seq", "sub"), axis=0, tiled=True)
    row_count = key_piece.shape[0]
    block_size = math.gcd(row_count, 512)
    turn_count = row_count // block_size
    key_blocks = key_piece.reshape(turn_count, block_size, local_heads, HD)
    value_blocks = value_piece.reshape(turn_count, block_size, local_heads, HD)

    def advance(state, block_pair):
        key_block, value_block = block_pair
        highest, weight_sum, weighted = state
        scores = (
            jnp.einsum("hqd,khd->hqk", q_heads, key_block, preferred_element_type=jnp.float32)
            * factor
        )
        new_high = jnp.maximum(highest, jnp.max(scores, axis=-1))
        shrink = jnp.exp(highest - new_high)
        weights = jnp.exp(scores - new_high[..., None])
        new_sum = weight_sum * shrink + jnp.sum(weights, axis=-1)
        probs = weights.astype(jnp.bfloat16)
        added = jnp.einsum("hqk,khd->hqd", probs, value_block, preferred_element_type=jnp.float32)
        return ((new_high, new_sum, weighted * shrink[..., None] + added), None)

    partial_value = lax.scan(advance, initial, (key_blocks, value_blocks))[0]
    weight_sum = partial_value[1]
    weighted = partial_value[2]
    result = weighted / weight_sum[..., None]
    outputs = result.transpose(1, 0, 2).reshape(half_rows, local_heads * HD).astype(jnp.bfloat16)
    return lax.all_to_all(outputs, "head", split_axis=0, concat_axis=1, tiled=True)


def solution(mesh):
    in_specs = (
        P(("grp", "seq", "head", "sub"), None),
        P(("grp", "seq", "head", "sub"), None),
        P(("grp", "seq", "head", "sub"), None),
        P(),
        P(),
    )
    out_specs = P(("grp", "seq", "head", "sub"), None)
    return jax.shard_map(body, mesh=mesh, in_specs=in_specs, out_specs=out_specs, check_vma=False)
```

profile of v0, /device:TPU:0, one launch (start us, length us, event | category | flops | bytes accessed | tf_op | source)
XLA Modules:
  0.0 108.0 jit_solution(10044975855559807415)
XLA Ops:
  6.5 0.0 copy-start.1
  6.5 0.0 copy-start
  6.5 0.0 copy-start.2
  6.5 0.0 all-gather.3.cloned.1.call-start
  6.5 1.2 %fusion.12 = f32[24]{0:T(128)S(1)} fusion(bf16[24,5120]{1,0:T(8,128)(2,1)} %param.8), kind=kLoop, calls=%fused_computation.22 | loop fusion | flops 368616 | bytes 245856 | tf_op jit(solution)/shard_map/reduce_sum | solution.py:16
  7.7 1.1 %fusion.14 = bf16[24,5120]{1,0:T(8,128)(2,1)S(1)} fusion(bf16[24,5120]{1,0:T(8,128)(2,1)} %param.8, f32[5120]{0:T(1024)} %param.11, f32[24]{0:T(128)S(1)} %add_rsqrt_fusion.1), kind=kLoop, calls=%fused_computation.24 | loop fusion | flops 491520 | bytes 512096 | tf_op jit(solution)/shard_map/convert_element_type | solution.py:17
  8.8 9.6 %all_to_all.70 = bf16[24,2,2560]{2,0,1:T(8,128)(2,1)} all-to-all(bf16[24,2,2560]{2,0,1:T(8,128)(2,1)S(1)} %bitcast.48), channel_id=1, replica_groups=mesh['grp'=2,'seq'=4,'head'=2,'sub'=2] {'head'}, dimensions={1} | all-to-all | bytes 491520 | tf_op jit(solution)/shard_map/all_to_all | solution.py:25
  18.4 0.0 all-gather.3.cloned.1.call-update
  18.4 0.0 all-gather.5.cloned.1.call-start
  18.5 0.0 copy-done.1
  18.5 8.2 %all_to_all.71 = bf16[24,2,2560]{2,0,1:T(8,128)(2,1)} all-to-all(bf16[24,2,2560]{2,0,1:T(8,128)(2,1)S(1)} %bitcast.50), channel_id=1, replica_groups=mesh['grp'=2,'seq'=4,'head'=2,'sub'=2] {'head'}, dimensions={1} | all-to-all | bytes 491520 | tf_op jit(solution)/shard_map/all_to_all | solution.py:26
  26.7 0.0 all-gather.5.cloned.1.call-update
  26.7 0.0 copy-done
  26.7 0.2 fusion.15
  26.9 0.0 copy-done.2
  26.9 0.1 fusion.17
  27.0 0.7 copy.35
  27.7 3.4 %all-to-all-start.1 = ((bf16[24,2,2560]{2,0,1:T(8,128)(2,1)}), bf16[24,2,2560]{2,0,1:T(8,128)(2,1)S(1)}, u32[]{:S(2)}, u32[]{:S(2)}) async-start(bf16[24,2,2560]{2,0,1:T(8,128)(2,1)} %bitcast.34), calls=%async_computation.1 | async-start | bytes 491520 | tf_op jit(solution)/shard_map/all_to_all | solution.py:24
  31.2 5.0 %all-to-all-done.1 = bf16[24,2,2560]{2,0,1:T(8,128)(2,1)S(1)} async-done(((bf16[24,2,2560]{2,0,1:T(8,128)(2,1)}), bf16[24,2,2560]{2,0,1:T(8,128)(2,1)S(1)}, u32[]{:S(2)}, u32[]{:S(2)}) %all-to-all-start.1) | async-done | bytes 245792 | tf_op jit(solution)/shard_map/all_to_all | solution.py:24
  36.3 0.2 reshape.47
  36.5 10.7 %all-gather.3.cloned.1.call-done = bf16[384,2560]{1,0:T(8,128)(2,1)} async-done(((bf16[48,2560]{1,0:T(8,128)(2,1)}), bf16[384,2560]{1,0:T(8,128)(2,1)}) %all-gather.3.cloned.1.call-update) | async-done | bytes 1966096 | tf_op jit(solution)/shard_map/all_gather | solution.py:38
  47.2 4.3 %reshape.46 = bf16[3,128,20,128]{3,2,1,0:T(8,128)(2,1)} reshape(bf16[384,2560]{1,0:T(8,128)(2,1)} %all-gather.3.cloned.1.call-done) | data formatting | bytes 3932160 | tf_op jit(solution)/shard_map/reshape | solution.py:43
  51.5 2.1 %copy.22 = bf16[3,128,20,128]{3,1,2,0:T(8,128)(2,1)S(1)} copy(bf16[3,128,20,128]{3,2,1,0:T(8,128)(2,1)} %reshape.46) | data formatting | bytes 3932160
  53.7 22.7 %all-gather.5.cloned.1.call-done = bf16[384,2560]{1,0:T(8,128)(2,1)} async-done(((bf16[48,2560]{1,0:T(8,128)(2,1)}), bf16[384,2560]{1,0:T(8,128)(2,1)}) %all-gather.5.cloned.1.call-update) | async-done | bytes 1966096 | tf_op jit(solution)/shard_map/all_gather | solution.py:39
  76.4 4.3 %reshape.48 = bf16[3,128,20,128]{3,2,1,0:T(8,128)(2,1)} reshape(bf16[384,2560]{1,0:T(8,128)(2,1)} %all-gather.5.cloned.1.call-done) | data formatting | bytes 3932160 | tf_op jit(solution)/shard_map/reshape | solution.py:44
  80.7 3.4 %copy.24 = bf16[3,128,20,128]{3,1,2,0:T(8,128)(2,1)} copy(bf16[3,128,20,128]{3,2,1,0:T(8,128)(2,1)} %reshape.48) | data formatting | bytes 3932160
  84.1 7.8 %while.15 = (s32[]{:T(128)}, f32[20,48]{1,0:T(8,128)S(1)}, f32[20,48]{1,0:T(8,128)S(1)}, f32[20,48,128]{2,1,0:T(8,128)S(1)}, bf16[3,128,20,128]{3,1,2,0:T(8,128)...) while((s32[]{:T(128)}, f32[20,48]{1,0:T(8,128)S(1)}, ...), condition=%wide.region_5.6_spmd.clone, body=%wide.region_2.5_spmd.clone.sunk | while | flops 64025280 | bytes 4076141 | solution.py:61
  84.1 0.6 fusion.30
  84.8 0.4 fusion.31
  85.2 1.5 %convolution_add_fusion.2 = f32[20,48,128]{2,1,0:T(8,128)S(1)} fusion(bf16[3,128,20,128]{3,1,2,0:T(8,128)(2,1)} %get-tuple-element.183, s32[]{:T(128)} %get-tuple-element.168, f32[20,48,128]{2,1,0:T(8,128)S(1)} %get-tuple-element.171, f32[20,48,128]{2,1,0:T(8,128)S(1)} %get-tuple-element.156, f32[20,48]{1,0:T(8,128)S(1)} %get-tuple-element.158, ...), kind=kOutput, calls=%fused_computation.clone.1 | convolution fusion | flops 32071680 | bytes 2138113 | tf_op jit(solution)/shard_map/while/body/eval_jaxpr/hqk,khd->hqd/dot_general | solution.py:58
  86.7 0.6 fusion.30
  87.4 0.4 fusion.31
  87.8 1.5 %convolution_add_fusion.2 = f32[20,48,128]{2,1,0:T(8,128)S(1)} fusion(bf16[3,128,20,128]{3,1,2,0:T(8,128)(2,1)} %get-tuple-element.183, s32[]{:T(128)} %get-tuple-element.168, f32[20,48,128]{2,1,0:T(8,128)S(1)} %get-tuple-element.171, f32[20,48,128]{2,1,0:T(8,128)S(1)} %get-tuple-element.156, f32[20,48]{1,0:T(8,128)S(1)} %get-tuple-element.158, ...), kind=kOutput, calls=%fused_computation.clone.1 | convolution fusion | flops 32071680 | bytes 2138113 | tf_op jit(solution)/shard_map/while/body/eval_jaxpr/hqk,khd->hqd/dot_general | solution.py:58
  89.3 0.6 fusion.30
  90.0 0.4 fusion.31
  90.4 1.5 %convolution_add_fusion.2 = f32[20,48,128]{2,1,0:T(8,128)S(1)} fusion(bf16[3,128,20,128]{3,1,2,0:T(8,128)(2,1)} %get-tuple-element.183, s32[]{:T(128)} %get-tuple-element.168, f32[20,48,128]{2,1,0:T(8,128)S(1)} %get-tuple-element.171, f32[20,48,128]{2,1,0:T(8,128)S(1)} %get-tuple-element.156, f32[20,48]{1,0:T(8,128)S(1)} %get-tuple-element.158, ...), kind=kOutput, calls=%fused_computation.clone.1 | convolution fusion | flops 32071680 | bytes 2138113 | tf_op jit(solution)/shard_map/while/body/eval_jaxpr/hqk,khd->hqd/dot_general | solution.py:58
  91.9 0.2 fusion.18
  92.1 0.1 copy.25
  92.2 0.2 convert_element_type.31
  92.4 8.0 %all_to_all.72 = bf16[2,24,2560]{2,1,0:T(8,128)(2,1)S(1)} all-to-all(bf16[2,24,2560]{2,1,0:T(8,128)(2,1)S(1)} %convert_element_type.31), channel_id=1, replica_groups=mesh['grp'=2,'seq'=4,'head'=2,'sub'=2] {'head'}, dimensions={0} | all-to-all | bytes 491520 | tf_op jit(solution)/shard_map/all_to_all | solution.py:66
  100.4 0.7 copy.30
  (17 shorter events, 0.2 us)
Async XLA Ops:
  6.5 11.9 %copy-start.1 = (bf16[24,5120]{1,0:T(8,128)(2,1)S(1)}, bf16[24,5120]{1,0:T(8,128)(2,1)}, u32[]{:S(2)}) copy-start(bf16[24,5120]{1,0:T(8,128)(2,1)} %param.9) | copy-start | bytes 737284
  6.5 20.2 %copy-start = (bf16[24,5120]{1,0:T(8,128)(2,1)S(1)}, bf16[24,5120]{1,0:T(8,128)(2,1)}, u32[]{:S(2)}) copy-start(bf16[24,5120]{1,0:T(8,128)(2,1)} %param.7) | copy-start | bytes 737284
  6.5 20.3 %copy-start.2 = (f32[5120]{0:T(1024)S(1)}, f32[5120]{0:T(1024)}, u32[]{:S(2)}) copy-start(f32[5120]{0:T(1024)} %param.10) | copy-start | bytes 61444
  6.5 40.7 %all-gather.3.cloned.1.call-start = ((), (), s32[]{:S(2)}) async-start(), calls=%async_computation.4 | async-start | bytes 2211840 | tf_op jit(solution)/shard_map/all_gather | solution.py:38
  18.4 57.9 %all-gather.5.cloned.1.call-start = ((), (), s32[]{:S(2)}) async-start(), calls=%async_computation.5 | async-start | bytes 2211840 | tf_op jit(solution)/shard_map/all_gather | solution.py:39
  27.7 8.5 %all-to-all-start.1 = ((bf16[24,2,2560]{2,0,1:T(8,128)(2,1)}), bf16[24,2,2560]{2,0,1:T(8,128)(2,1)S(1)}, u32[]{:S(2)}, u32[]{:S(2)}) async-start(bf16[24,2,2560]{2,0,1:T(8,128)(2,1)} %bitcast.34), calls=%async_computation.1 | async-start | bytes 491520 | tf_op jit(solution)/shard_map/all_to_all | solution.py:24
Sparse Core Ops, SparseCore 0:
  18.5 28.6 all-gather.2
  48.8 27.4 all-gather.4
where the time goes:
time: 109 us; the launch traced here: 108 us
  waiting for transfers between devices  38.5 us (35%)
  blocking collectives  25.8 us (24%)
  local copies, waits for them, and re-layouts  16.2 us (15%)
  between operations  13.5 us (12%)
  matrix products  6.39 us (6%)
  other arithmetic  3.95 us (4%)
  starting transfers between devices  3.48 us (3%)
    all_gather x1, waiting for transfers between devices, body(): value_piece = lax.all_gather(v_local, ('seq', 'sub'), axis=0, tiled=True)  22.7 us
    all_gather x1, waiting for transfers between devices, body(): key_piece = lax.all_gather(k_local, ('seq', 'sub'), axis=0, tiled=True)  10.7 us
    all_to_all x1, blocking collectives, body(): lax.all_to_all(k_normed, 'head', split_axis=1, concat_axis=0, tiled=True)  9.57 us
    all_to_all x1, blocking collectives, body(): lax.all_to_all(values, 'head', split_axis=1, concat_axis=0, tiled=True)  8.16 us
    all_to_all x1, blocking collectives, body(): lax.all_to_all(outputs, 'head', split_axis=0, concat_axis=1, tiled=True)  8.04 us
    unnamed x9, local copies, waits for them, and re-layouts  5.64 us
    all_to_all x1, waiting for transfers between devices, body(): lax.all_to_all(q_normed, 'head', split_axis=1, concat_axis=0, tiled=True)  5.04 us
    dot_general x3, matrix products, advance(): jnp.einsum('hqk,khd->hqd', probs, value_block, preferred_element_type=jnp...  4.47 us
  transfers between devices with their start and end apart: 3, of which 3 were waited for; matrix products, arithmetic and copies ran while one was open for 7% of the time, Pallas kernels for 0%

commit v1 on v0

--- a/solution.py
+++ b/solution.py
@@ -1,8 +1,11 @@
+import functools
 import math
 
 import jax
 import jax.numpy as jnp
 from jax import lax
+from jax.experimental import pallas as pl
+from jax.experimental.pallas import tpu as pltpu
 from jax.sharding import PartitionSpec as P
 
 HD = 128
@@ -17,7 +20,7 @@
     return (widened * inverse * gain).astype(jnp.bfloat16)
 
 
-def body(queries, keys, values, q_gain, k_gain):
+def gathered_body(queries, keys, values, q_gain, k_gain):
     q_normed = normalize(queries, q_gain)
     k_normed = normalize(keys, k_gain)
     q_local, k_local, v_local = (
@@ -66,13 +69,82 @@
     return lax.all_to_all(outputs, "head", split_axis=0, concat_axis=1, tiled=True)
 
 
+CHIP = ("seq", "head")
+
+
+def pack_kernel(chips, q_ref, k_ref, v_ref, qg_ref, kg_ref, out_ref):
+    rows, width = q_ref.shape
+    part = width // chips
+    q_normed = normalize(q_ref[...], qg_ref[...])
+    k_normed = normalize(k_ref[...], kg_ref[...])
+    for chip in range(chips):
+        columns = slice(chip * part, (chip + 1) * part)
+        out_ref[chip, 0:rows, :] = v_ref[:, columns]
+        out_ref[chip, rows : 2 * rows, :] = k_normed[:, columns]
+        out_ref[chip, 2 * rows : 3 * rows, :] = q_normed[:, columns]
+
+
+def attend_kernel(chips, rows, mine_ref, other_ref, out_ref):
+    heads = mine_ref.shape[2] // HD
+    factor = 1.0 / math.sqrt(HD)
+
+    def joined(refs, first, columns):
+        pieces = [
+            ref[chip, first : first + rows, columns].astype(jnp.float32)
+            for ref in refs
+            for chip in range(chips)
+        ]
+        return jnp.concatenate(pieces, axis=0).astype(jnp.bfloat16)
+
+    for head in range(heads):
+        columns = slice(head * HD, (head + 1) * HD)
+        v_head = joined((mine_ref, other_ref), 0, columns)
+        k_head = joined((mine_ref, other_ref), rows, columns)
+        q_head = joined((mine_ref,), 2 * rows, columns)
+        scores = (
+            lax.dot_general(
+                q_head, k_head, (((1,), (1,)), ((), ())), preferred_element_type=jnp.float32
+            )
+            * factor
+        )
+        highest = jnp.max(scores, axis=-1, keepdims=True)
+        weights = jnp.exp(scores - highest)
+        weight_sum = jnp.sum(weights, axis=-1, keepdims=True)
+        weighted = jnp.dot(weights.astype(jnp.bfloat16), v_head, preferred_element_type=jnp.float32)
+        result = (weighted / weight_sum).astype(jnp.bfloat16)
+        for chip in range(chips):
+            out_ref[chip, :, columns] = result[chip * rows : (chip + 1) * rows, :]
+
+
+def split_body(chips, queries, keys, values, q_gain, k_gain):
+    rows, width = queries.shape
+    part = width // chips
+    packed = pl.pallas_call(
+        functools.partial(pack_kernel, chips),
+        out_shape=jax.ShapeDtypeStruct((chips, 3 * rows, part), jnp.bfloat16),
+    )(queries, keys, values, q_gain[None, :], k_gain[None, :])
+    mine = lax.all_to_all(packed, CHIP, split_axis=0, concat_axis=0, tiled=True)
+    swap = [(0, 1), (1, 0)]
+    other = lax.ppermute(mine[:, : 2 * rows], "sub", swap)
+    attended = pl.pallas_call(
+        functools.partial(attend_kernel, chips, rows),
+        out_shape=jax.ShapeDtypeStruct((chips, rows, part), jnp.bfloat16),
+    )(mine, other)
+    back = lax.all_to_all(attended, CHIP, split_axis=0, concat_axis=0, tiled=True)
+    return back.transpose(1, 0, 2).reshape(rows, width)
+
+
 def solution(mesh):
-    in_specs = (
-        P(("grp", "seq", "head", "sub"), None),
-        P(("grp", "seq", "head", "sub"), None),
-        P(("grp", "seq", "head", "sub"), None),
-        P(),
-        P(),
+    chips = mesh.shape["seq"] * mesh.shape["head"]
+
+    def body(queries, *rest):
+        heads = queries.shape[1] // HD
+        if heads % chips or mesh.shape["sub"] != 2:
+            return gathered_body(queries, *rest)
+        return split_body(chips, queries, *rest)
+
+    token_spec = P(("grp", "seq", "head", "sub"), None)
+    in_specs = (token_spec, token_spec, token_spec, P(), P())
+    return jax.shard_map(
+        body, mesh=mesh, in_specs=in_specs, out_specs=token_spec, check_vma=False
     )
-    out_specs = P(("grp", "seq", "head", "sub"), None)
-    return jax.shard_map(body, mesh=mesh, in_specs=in_specs, out_specs=out_specs, check_vma=False)

time: 109 us -> 48.6 us (0.45)
  waiting for transfers between devices: 38.5 us -> 1.85 us
  local copies, waits for them, and re-layouts: 16.2 us -> 1.54 us
  between operations: 13.5 us -> 0.02 us
  blocking collectives: 25.8 us -> 38.9 us
  matrix products: 6.39 us -> 0 us
  Pallas kernels: 0 us -> 5.8 us
  other arithmetic: 3.95 us -> 0 us
  starting transfers between devices: 3.48 us -> 0.07 us
    all_gather x2 -> x0, waiting for transfers between devices: 33.4 us -> none  [the longest x1 22.7 us: body(): value_piece = lax.all_gather(v_local, ('seq', 'sub'), axis=0, tiled=True)]
    all_to_all x3 -> x2, blocking collectives: 25.8 us -> 38.9 us  [the longest x1 26.4 us: split_body(): mine = lax.all_to_all(packed, CHIP, split_axis=0, concat_axis=0, tiled=True)]
    reshape x3 -> x1, local copies, waits for them, and re-layouts: 8.85 us -> 0.71 us  [split_body(): return back.transpose(1, 0, 2).reshape(rows, width)]
    dot_general x6 -> x0, matrix products: 6.39 us -> none  [the longest x3 4.47 us: advance(): jnp.einsum('hqk,khd->hqd', probs, value_block, preferred_element_type=jnp...]
    pallas_call x0 -> x2, Pallas kernels: none -> 5.8 us  [the longest x1 3.47 us: split_body(): pl.pallas_call(functools.partial(attend_kernel, chips, rows), out_shape=j...]
    all_to_all x1 -> x0, waiting for transfers between devices: 5.04 us -> none  [body(): lax.all_to_all(q_normed, 'head', split_axis=1, concat_axis=0, tiled=True)]
    unnamed x9 -> x4, local copies, waits for them, and re-layouts: 5.64 us -> 0.78 us
    all_to_all x1 -> x0, starting transfers between devices: 3.44 us -> none  [body(): lax.all_to_all(q_normed, 'head', split_axis=1, concat_axis=0, tiled=True)]
  transfers between devices with their start and end apart: 3 -> 1, of which waited for: 3 -> 1; matrix products, arithmetic and copies ran while one was open for 7% -> 0% of each run, Pallas kernels for 0% -> 0%
where the time goes in v1:
time: 48.6 us; the launch traced here: 48.2 us
  blocking collectives  38.9 us (80%)
  Pallas kernels  5.8 us (12%)
  waiting for transfers between devices  1.85 us (4%)
  local copies, waits for them, and re-layouts  1.54 us (3%)
    all_to_all x1, blocking collectives, split_body(): mine = lax.all_to_all(packed, CHIP, split_axis=0, concat_axis=0, tiled=True)  26.4 us
    all_to_all x1, blocking collectives, split_body(): lax.all_to_all(attended, CHIP, split_axis=0, concat_axis=0, tiled=True)  12.6 us
    pallas_call x1, Pallas kernels, split_body(): pl.pallas_call(functools.partial(attend_kernel, chips, rows), out_shape=j...  3.47 us
    pallas_call x1, Pallas kernels, split_body(): pl.pallas_call(functools.partial(pack_kernel, chips), out_shape=jax.Shape...  2.32 us
    ppermute x1, waiting for transfers between devices, split_body(): other = lax.ppermute(mine[:, :2 * rows], 'sub', swap)  1.85 us
  transfers between devices with their start and end apart: 1, of which 1 were waited for; matrix products, arithmetic and copies ran while one was open for 0% of the time, Pallas kernels for 0%

profile of v1, /device:TPU:0, one launch (start us, length us, event | category | flops | bytes accessed | tf_op | source)
XLA Modules:
  0.0 48.2 jit_solution(15409170319485617851)
XLA Ops:
  0.0 2.3 %shard_map.55 = bf16[8,72,640]{2,1,0:T(8,128)(2,1)} custom-call(bf16[24,5120]{1,0:T(8,128)(2,1)} %q_ref.1, bf16[24,5120]{1,0:T(8,128)(2,1)} %k_ref.1, bf16[24,5120]{1,0:T(8,128)(2,1)} %v_ref.1, f32[1,5120]{1,0:T(1,128)} %bitcast.6, f32[1,5120]{1,0:T(1,128)} %bitcast.7), custom_call_target="tpu_custom_call" | custom-call | tf_op jit(solution)/shard_map/pallas_call | solution.py:122
  2.3 26.4 %all_to_all.10.mine_ref = bf16[8,72,640]{2,1,0:T(8,128)(2,1)S(1)} all-to-all(bf16[8,72,640]{2,1,0:T(8,128)(2,1)} %shard_map.55), channel_id=1, replica_groups=mesh['grp'=2,'seq'=4,'head'=2,'sub'=2] {'seq','head'}, dimensions={0} | all-to-all | bytes 1474560 | tf_op jit(solution)/shard_map/all_to_all | solution.py:126
  28.7 0.0 copy-start
  28.7 0.1 collective-permute-start
  28.8 1.9 %collective-permute-done.other_ref = bf16[8,48,640]{2,1,0:T(8,128)(2,1)S(1)} collective-permute-done((bf16[8,48,640]{2,1,0:T(8,128)(2,1)S(1)}, bf16[8,48,640]{2,1,0:T(8,128)(2,1)S(1)}, u32[]{:S(2)}, u32[]{:S(2)}) %collective-permute-start) | collective-permute-done | bytes 491552 | tf_op jit(solution)/shard_map/ppermute | solution.py:128
  30.7 0.0 copy-done
  30.7 0.0 copy-start.1
  30.7 0.8 %copy-done.1 = bf16[8,48,640]{2,1,0:T(8,128)(2,1)} copy-done((bf16[8,48,640]{2,1,0:T(8,128)(2,1)}, bf16[8,48,640]{2,1,0:T(8,128)(2,1)S(1)}, u32[]{:S(2)}) %copy-start.1) | copy-done | bytes 491544
  31.5 3.5 %shard_map.56 = bf16[8,24,640]{2,1,0:T(8,128)(2,1)} custom-call(bf16[8,72,640]{2,1,0:T(8,128)(2,1)} %copy-done, bf16[8,48,640]{2,1,0:T(8,128)(2,1)} %copy-done.1), custom_call_target="tpu_custom_call" | custom-call | tf_op jit(solution)/shard_map/pallas_call | solution.py:129
  34.9 12.6 %all_to_all.11 = bf16[8,24,640]{2,1,0:T(8,128)(2,1)S(1)} all-to-all(bf16[8,24,640]{2,1,0:T(8,128)(2,1)} %shard_map.56), channel_id=1, replica_groups=mesh['grp'=2,'seq'=4,'head'=2,'sub'=2] {'seq','head'}, dimensions={0} | all-to-all | bytes 491520 | tf_op jit(solution)/shard_map/all_to_all | solution.py:133
  47.5 0.7 %copy.7 = bf16[8,3,8,640]{3,2,0,1:T(8,128)(2,1)} copy(bf16[8,3,8,640]{3,2,1,0:T(8,128)(2,1)S(1)} %bitcast.5) | data formatting | bytes 491520 | tf_op jit(solution)/shard_map/reshape | solution.py:134
  (1 shorter events, 0.0 us)
Async XLA Ops:
  28.7 2.0 %copy-start = (bf16[8,72,640]{2,1,0:T(8,128)(2,1)}, bf16[8,72,640]{2,1,0:T(8,128)(2,1)S(1)}, u32[]{:S(2)}) copy-start(bf16[8,72,640]{2,1,0:T(8,128)(2,1)S(1)} %all_to_all.10.mine_ref) | copy-start | bytes 2211844
  28.7 1.9 %collective-permute-start = (bf16[8,48,640]{2,1,0:T(8,128)(2,1)S(1)}, bf16[8,48,640]{2,1,0:T(8,128)(2,1)S(1)}, u32[]{:S(2)}, u32[]{:S(2)}) collective-permute-start(bf16[8,48,640]{2,1,0:T(8,128)(2,1)S(1)} %slice.4), channel_id=1, source_target_pairs={{0,1},{1,0},{2,3},{3,2},{4,5},{5,4},{6,7},{7,6},{8,9},{9,8},{10,11... | collective-permute-start | bytes 1474568 | tf_op jit(solution)/shard_map/ppermute | solution.py:128
  30.7 0.8 %copy-start.1 = (bf16[8,48,640]{2,1,0:T(8,128)(2,1)}, bf16[8,48,640]{2,1,0:T(8,128)(2,1)S(1)}, u32[]{:S(2)}) copy-start(bf16[8,48,640]{2,1,0:T(8,128)(2,1)S(1)} %collective-permute-done.other_ref) | copy-start | bytes 1474564

commit v2 on v0

--- a/solution.py
+++ b/solution.py
@@ -1,9 +1,13 @@
+import functools
 import math
 
 import jax
 import jax.numpy as jnp
 from jax import lax
+from jax.experimental import pallas as pl
+from jax.experimental.pallas import tpu as pltpu
 from jax.sharding import PartitionSpec as P
+
 
 HD = 128
 
@@ -17,7 +21,7 @@
     return (widened * inverse * gain).astype(jnp.bfloat16)
 
 
-def body(queries, keys, values, q_gain, k_gain):
+def gathered_body(queries, keys, values, q_gain, k_gain):
     q_normed = normalize(queries, q_gain)
     k_normed = normalize(keys, k_gain)
     q_local, k_local, v_local = (
@@ -66,13 +70,195 @@
     return lax.all_to_all(outputs, "head", split_axis=0, concat_axis=1, tiled=True)
 
 
+CHIP = ("seq", "head")
+BF16 = jnp.bfloat16
+F32 = jnp.float32
+SWAP = [(0, 1), (1, 0)]
+
+
+def inverse_rms(ref):
+    widened = ref[...].astype(F32)
+    return lax.rsqrt(jnp.mean(widened * widened, axis=-1, keepdims=True) + EPS)
+
+
+def pack_kernel(groups, me_ref, *refs):
+    sources, outs, (q_ref, k_ref, v_ref, qg_ref, kg_ref, sems) = refs[:5], refs[5:-6], refs[-6:]
+    copies = [
+        pltpu.make_async_copy(source, target, sems.at[place])
+        for place, (source, target) in enumerate(zip(sources, refs[-6:-1]))
+    ]
+    for copy in copies:
+        copy.start()
+    for copy in copies:
+        copy.wait()
+    rows, width = q_ref.shape
+    part = width // groups
+    full_refs, far_refs = outs[:groups], outs[groups:]
+    q_inverse, k_inverse = inverse_rms(q_ref), inverse_rms(k_ref)
+    for step in range(groups):
+        group = lax.bitwise_xor(me_ref[0], step)
+        columns = pl.ds(pl.multiple_of(group * part, HD), part)
+        v_part = v_ref[:, columns]
+        k_part = (k_ref[:, columns].astype(F32) * k_inverse * kg_ref[:, columns]).astype(BF16)
+        q_part = (q_ref[:, columns].astype(F32) * q_inverse * qg_ref[:, columns]).astype(BF16)
+        full, far = full_refs[step], far_refs[step]
+        far[0:rows, :] = v_part
+        far[rows : 2 * rows, :] = k_part
+        full[0:rows, :] = v_part
+        full[rows : 2 * rows, :] = k_part
+        full[2 * rows : 3 * rows, :] = q_part
+
+
+def joined(refs, first, rows, columns):
+    pieces = [ref[first : first + rows, columns].astype(F32) for ref in refs]
+    return jnp.concatenate(pieces, axis=0).astype(BF16)
+
+
+def head_scores(q_head, k_head):
+    factor = 1.0 / math.sqrt(HD)
+    dims = (((1,), (1,)), ((), ()))
+    return lax.dot_general(q_head, k_head, dims, preferred_element_type=F32) * factor
+
+
+def columns_of(head):
+    return slice(head * HD, (head + 1) * HD)
+
+
+def all_scores(query_refs, key_refs):
+    rows, heads = query_refs[0].shape[0] // 3, query_refs[0].shape[1] // HD
+    scores = []
+    for head in range(heads):
+        q_head = joined(query_refs, 2 * rows, rows, columns_of(head))
+        scores.append(head_scores(q_head, joined(key_refs, rows, rows, columns_of(head))))
+    return scores
+
+
+def near_kernel(groups, *refs):
+    near, (high_ref, sum_ref, acc_ref) = refs[:-3], refs[-3:]
+    rows = near[0].shape[0] // 3
+    all_weights = []
+    for head, scores in enumerate(all_scores(near[:groups], near)):
+        highest = jnp.max(scores, axis=-1, keepdims=True)
+        weights = jnp.exp(scores - highest)
+        high_ref[head] = jnp.broadcast_to(highest, high_ref.shape[1:])
+        weight_sum = jnp.sum(weights, axis=-1, keepdims=True)
+        sum_ref[head] = jnp.broadcast_to(weight_sum, sum_ref.shape[1:])
+        all_weights.append(weights.astype(BF16))
+    for head, weights in enumerate(all_weights):
+        v_head = joined(near, 0, rows, columns_of(head))
+        acc_ref[head] = jnp.dot(weights, v_head, preferred_element_type=F32)
+
+
+def far_kernel(groups, high_ref, sum_ref, acc_ref, *refs):
+    near, far, outs = refs[:groups], refs[groups : 3 * groups], refs[3 * groups :]
+    rows = near[0].shape[0] // 3
+    kept = []
+    for head, scores in enumerate(all_scores(near, far)):
+        before = high_ref[head]
+        highest = jnp.maximum(before, jnp.max(scores, axis=-1, keepdims=True))
+        weights = jnp.exp(scores - highest[:, 0:1])
+        shrink = jnp.exp(before - highest)
+        weight_sum = sum_ref[head] * shrink + jnp.sum(weights, axis=-1, keepdims=True)
+        kept.append((weights.astype(BF16), acc_ref[head] * shrink, weight_sum))
+    for head, (weights, acc, weight_sum) in enumerate(kept):
+        v_head = joined(far, 0, rows, columns_of(head))
+        added = jnp.dot(weights, v_head, preferred_element_type=F32)
+        result = ((acc + added) / weight_sum).astype(BF16)
+        for step in range(groups):
+            outs[step][:, columns_of(head)] = result[step * rows : (step + 1) * rows, :]
+
+
+def place_kernel(groups, me_ref, *refs):
+    parts, out_ref = refs[:-1], refs[-1]
+    part = parts[0].shape[1]
+    for step in range(groups):
+        group = lax.bitwise_xor(me_ref[0], step)
+        out_ref[:, pl.ds(pl.multiple_of(group * part, HD), part)] = parts[step][...]
+
+
+def kernel_call(kernel, shapes, scalars=0, fetched=(), scratch=(), limit=16 << 20):
+    smem = pl.BlockSpec(memory_space=pltpu.SMEM)
+    vmem = pl.BlockSpec(memory_space=pltpu.VMEM)
+    hbm = pl.BlockSpec(memory_space=pltpu.HBM)
+
+    def call(*args):
+        places = [smem if i < scalars else hbm if i in fetched else vmem for i in range(len(args))]
+        return pl.pallas_call(
+            kernel,
+            out_shape=shapes,
+            in_specs=places,
+            out_specs=jax.tree.map(lambda _: vmem, shapes),
+            scratch_shapes=scratch,
+            compiler_params=pltpu.CompilerParams(vmem_limit_bytes=limit),
+        )(*args)
+
+    return call
+
+
+def halves_body(sizes, queries, keys, values, q_gain, k_gain):
+    seq, across = sizes["seq"], sizes["head"]
+    groups = seq // 2 * across
+    rows, width = queries.shape
+    part = width // groups
+    heads = part // HD
+    me = lax.axis_index("seq") % (seq // 2) * across + lax.axis_index("head")
+    me = me.astype(jnp.int32).reshape(1)
+
+    def send(value, half, step):
+        place = half * (seq // 2) * across + step
+        return lax.ppermute(value, CHIP, [(i, i ^ place) for i in range(seq * across)])
+
+    def swap(value):
+        return lax.ppermute(value, "sub", SWAP)
+
+    steps = range(groups)
+    full = jax.ShapeDtypeStruct((3 * rows, part), BF16)
+    far = jax.ShapeDtypeStruct((2 * rows, part), BF16)
+    token = pltpu.VMEM((rows, width), BF16)
+    gain = pltpu.VMEM((1, width), F32)
+    packed = kernel_call(
+        functools.partial(pack_kernel, groups),
+        [full] * groups + [far] * groups,
+        scalars=1,
+        fetched=range(1, 6),
+        limit=60 << 20,
+        scratch=[token] * 3 + [gain] * 2 + [pltpu.SemaphoreType.DMA((5,))],
+    )(me, queries, keys, values, q_gain[None, :], k_gain[None, :])
+    fulls, fars = packed[:groups], packed[groups:]
+    far_in = [send(fars[step], 1, step) for step in steps]
+    near_in = [fulls[0]] + [send(fulls[step], 0, step) for step in steps[1:]]
+    near_other = [swap(near_in[step]) for step in steps]
+    far_other = [swap(far_in[step]) for step in steps]
+    state = jax.ShapeDtypeStruct((heads, groups * rows, HD), F32)
+    partial = kernel_call(functools.partial(near_kernel, groups), [state] * 3)(
+        *near_in, *near_other
+    )
+    piece = jax.ShapeDtypeStruct((rows, part), BF16)
+    pieces = kernel_call(functools.partial(far_kernel, groups), [piece] * groups)(
+        *partial, *near_in, *far_in, *far_other
+    )
+    back = [pieces[0]] + [send(pieces[step], 0, step) for step in steps[1:]]
+    whole = jax.ShapeDtypeStruct((rows, width), BF16)
+    return kernel_call(functools.partial(place_kernel, groups), whole, scalars=1)(me, *back)
+
+
+def power_of_two(size):
+    return size & (size - 1) == 0
+
+
 def solution(mesh):
-    in_specs = (
-        P(("grp", "seq", "head", "sub"), None),
-        P(("grp", "seq", "head", "sub"), None),
-        P(("grp", "seq", "head", "sub"), None),
-        P(),
-        P(),
-    )
-    out_specs = P(("grp", "seq", "head", "sub"), None)
-    return jax.shard_map(body, mesh=mesh, in_specs=in_specs, out_specs=out_specs, check_vma=False)
+    sizes = mesh.shape
+    groups = sizes["seq"] // 2 * sizes["head"]
+    paired = sizes["sub"] == 2 and sizes["seq"] > 1
+    paired = paired and power_of_two(sizes["seq"]) and power_of_two(sizes["head"])
+
+    def body(queries, *rest):
+        if paired and queries.shape[1] // HD % groups == 0:
+            return halves_body(sizes, queries, *rest)
+        return gathered_body(queries, *rest)
+
+    token_spec = P(("grp", "seq", "head", "sub"), None)
+    in_specs = (token_spec, token_spec, token_spec, P(), P())
+    return jax.shard_map(
+        body, mesh=mesh, in_specs=in_specs, out_specs=token_spec, check_vma=False
+    )

time: 109 us -> 44.5 us (0.41)
  blocking collectives: 25.8 us -> 0 us
  waiting for transfers between devices: 38.5 us -> 19.7 us
  local copies, waits for them, and re-layouts: 16.2 us -> 0.92 us
  starting transfers between devices: 3.48 us -> 18.7 us
  between operations: 13.5 us -> 0.07 us
  matrix products: 6.39 us -> 0 us
  Pallas kernels: 0 us -> 4.95 us
  other arithmetic: 3.95 us -> 0 us
    all_gather x2 -> x0, waiting for transfers between devices: 33.4 us -> none  [the longest x1 22.7 us: body(): value_piece = lax.all_gather(v_local, ('seq', 'sub'), axis=0, tiled=True)]
    all_to_all x3 -> x0, blocking collectives: 25.8 us -> none  [the longest x1 9.57 us: body(): lax.all_to_all(k_normed, 'head', split_axis=1, concat_axis=0, tiled=True)]
    ppermute x0 -> x18, waiting for transfers between devices: none -> 19.7 us  [the longest x10 19.7 us: send(): lax.ppermute(value, CHIP, [(i, i ^ place) for i in range(seq * across)])]
    ppermute x0 -> x18, starting transfers between devices: none -> 18.7 us  [the longest x10 17 us: send(): lax.ppermute(value, CHIP, [(i, i ^ place) for i in range(seq * across)])]
    reshape x3 -> x0, local copies, waits for them, and re-layouts: 8.85 us -> none  [the longest x1 4.34 us: body(): key_blocks = key_piece.reshape(turn_count, block_size, local_heads, HD)]
    dot_general x6 -> x0, matrix products: 6.39 us -> none  [the longest x3 4.47 us: advance(): jnp.einsum('hqk,khd->hqd', probs, value_block, preferred_element_type=jnp...]
    all_to_all x1 -> x0, waiting for transfers between devices: 5.04 us -> none  [body(): lax.all_to_all(q_normed, 'head', split_axis=1, concat_axis=0, tiled=True)]
    pallas_call x0 -> x4, Pallas kernels: none -> 4.95 us  [call(): pl.pallas_call(kernel, out_shape=shapes, in_specs=places, out_specs=jax.t...]
  transfers between devices with their start and end apart: 3 -> 18, of which waited for: 3 -> 6; matrix products, arithmetic and copies ran while one was open for 7% -> 0% of each run, Pallas kernels for 0% -> 2%
where the time goes in v2:
time: 44.5 us; the launch traced here: 44.4 us
  waiting for transfers between devices  19.7 us (44%)
  starting transfers between devices  18.7 us (42%)
  Pallas kernels  4.95 us (11%)
  local copies, waits for them, and re-layouts  0.92 us (2%)
    ppermute x10, waiting for transfers between devices, send(): lax.ppermute(value, CHIP, [(i, i ^ place) for i in range(seq * across)])  19.7 us
    ppermute x10, starting transfers between devices, send(): lax.ppermute(value, CHIP, [(i, i ^ place) for i in range(seq * across)])  17 us
    pallas_call x4, Pallas kernels, call(): pl.pallas_call(kernel, out_shape=shapes, in_specs=places, out_specs=jax.t...  4.95 us
    ppermute x8, starting transfers between devices, swap(): return lax.ppermute(value, 'sub', SWAP)  1.76 us
    unnamed x2, local copies, waits for them, and re-layouts  0.92 us
  transfers between devices with their start and end apart: 18, of which 6 were waited for; matrix products, arithmetic and copies ran while one was open for 0% of the time, Pallas kernels for 2%

profile of v2, /device:TPU:0, one launch (start us, length us, event | category | flops | bytes accessed | tf_op | source)
XLA Modules:
  0.0 44.4 jit_solution(14262217016511323844)
XLA Ops:
  0.0 2.5 %shard_map.55 = (bf16[72,1280]{1,0:T(8,128)(2,1)}, bf16[72,1280]{1,0:T(8,128)(2,1)}, bf16[72,1280]{1,0:T(8,128)(2,1)}, bf16[72,1280]{1,0:T(8,128)(2,1)}, bf16[48...) custom-call(s32[1]{0:T(128)} %bitcast.me_ref, ...), custom_call_target="tpu_custom_call" | custom-call | tf_op jit(solution)/shard_map/pallas_call | solution.py:186
  2.5 4.1 %collective-permute-start.7 = (bf16[48,1280]{1,0:T(8,128)(2,1)}, bf16[48,1280]{1,0:T(8,128)(2,1)S(1)}, u32[]{:S(2)}, u32[]{:S(2)}) collective-permute-start(bf16[48,1280]{1,0:T(8,128)(2,1)} %get-tuple-element.27), channel_id=1, source_target_pairs={{0,8},{2,10},{4,12},{6,14},{8,0},{10,2},{12,4},{14,6},{1,9},{3,11}... | collective-permute-start | bytes 368648 | tf_op jit(solution)/shard_map/ppermute | solution.py:209
  6.6 1.5 %collective-permute-start = (bf16[72,1280]{1,0:T(8,128)(2,1)}, bf16[72,1280]{1,0:T(8,128)(2,1)S(1)}, u32[]{:S(2)}, u32[]{:S(2)}) collective-permute-start(bf16[72,1280]{1,0:T(8,128)(2,1)} %get-tuple-element.21), channel_id=1, source_target_pairs={{0,2},{2,0},{4,6},{6,4},{8,10},{10,8},{12,14},{14,12},{1,3},{3,1},... | collective-permute-start | bytes 552968 | tf_op jit(solution)/shard_map/ppermute | solution.py:209
  8.1 1.6 %collective-permute-start.1 = (bf16[72,1280]{1,0:T(8,128)(2,1)}, bf16[72,1280]{1,0:T(8,128)(2,1)S(1)}, u32[]{:S(2)}, u32[]{:S(2)}) collective-permute-start(bf16[72,1280]{1,0:T(8,128)(2,1)} %get-tuple-element.22), channel_id=1, source_target_pairs={{0,4},{2,6},{4,0},{6,2},{8,12},{10,14},{12,8},{14,10},{1,5},{3,7},... | collective-permute-start | bytes 552968 | tf_op jit(solution)/shard_map/ppermute | solution.py:209
  9.7 0.3 collective-permute-start.8
  10.0 2.5 %collective-permute-start.9 = (bf16[48,1280]{1,0:T(8,128)(2,1)}, bf16[48,1280]{1,0:T(8,128)(2,1)S(1)}, u32[]{:S(2)}, u32[]{:S(2)}) collective-permute-start(bf16[48,1280]{1,0:T(8,128)(2,1)} %get-tuple-element.29), channel_id=1, source_target_pairs={{0,12},{2,14},{4,8},{6,10},{8,4},{10,6},{12,0},{14,2},{1,13},{3,15... | collective-permute-start | bytes 368648 | tf_op jit(solution)/shard_map/ppermute | solution.py:209
  12.5 0.8 %collective-permute-done.7.refs_4_ = bf16[48,1280]{1,0:T(8,128)(2,1)S(1)} collective-permute-done((bf16[48,1280]{1,0:T(8,128)(2,1)}, bf16[48,1280]{1,0:T(8,128)(2,1)S(1)}, u32[]{:S(2)}, u32[]{:S(2)}) %collective-permute-start.7) | collective-permute-done | bytes 122912 | tf_op jit(solution)/shard_map/ppermute | solution.py:209
  13.3 1.4 %collective-permute-start.2 = (bf16[72,1280]{1,0:T(8,128)(2,1)}, bf16[72,1280]{1,0:T(8,128)(2,1)S(1)}, u32[]{:S(2)}, u32[]{:S(2)}) collective-permute-start(bf16[72,1280]{1,0:T(8,128)(2,1)} %get-tuple-element.23), channel_id=1, source_target_pairs={{0,6},{2,4},{4,2},{6,0},{8,14},{10,12},{12,10},{14,8},{1,7},{3,5},... | collective-permute-start | bytes 552968 | tf_op jit(solution)/shard_map/ppermute | solution.py:209
  14.7 8.3 %collective-permute-done.8.refs_5_ = bf16[48,1280]{1,0:T(8,128)(2,1)S(1)} collective-permute-done((bf16[48,1280]{1,0:T(8,128)(2,1)}, bf16[48,1280]{1,0:T(8,128)(2,1)S(1)}, u32[]{:S(2)}, u32[]{:S(2)}) %collective-permute-start.8) | collective-permute-done | bytes 122912 | tf_op jit(solution)/shard_map/ppermute | solution.py:209
  23.0 0.0 collective-permute-start.3
  23.0 0.0 collective-permute-done.refs_1_
  23.0 0.5 %collective-permute-start.4 = (bf16[72,1280]{1,0:T(8,128)(2,1)S(1)}, bf16[72,1280]{1,0:T(8,128)(2,1)S(1)}, u32[]{:S(2)}, u32[]{:S(2)}) collective-permute-start(bf16[72,1280]{1,0:T(8,128)(2,1)S(1)} %collective-permute-done.refs_1_), channel_id=1, source_target_pairs={{0,1},{1,0},{2,3},{3,2},{4,5},{5,4},{6,7},{7,6},{8,9},{9,8},{10,11... | collective-permute-start | bytes 552968 | tf_op jit(solution)/shard_map/ppermute | solution.py:212
  23.5 0.0 collective-permute-done.1.refs_2_
  23.5 0.1 collective-permute-start.5
  23.6 0.0 collective-permute-done.9.refs_6_
  23.6 2.1 %collective-permute-start.10 = (bf16[48,1280]{1,0:T(8,128)(2,1)}, bf16[48,1280]{1,0:T(8,128)(2,1)S(1)}, u32[]{:S(2)}, u32[]{:S(2)}) collective-permute-start(bf16[48,1280]{1,0:T(8,128)(2,1)} %get-tuple-element.30), channel_id=1, source_target_pairs={{0,14},{2,12},{4,10},{6,8},{8,6},{10,4},{12,2},{14,0},{1,15},{3,13... | collective-permute-start | bytes 368648 | tf_op jit(solution)/shard_map/ppermute | solution.py:209
  25.7 0.0 collective-permute-done.2.refs_3_
  25.7 0.2 collective-permute-start.6
  25.8 6.4 %collective-permute-done.10.refs_7_ = bf16[48,1280]{1,0:T(8,128)(2,1)S(1)} collective-permute-done((bf16[48,1280]{1,0:T(8,128)(2,1)}, bf16[48,1280]{1,0:T(8,128)(2,1)S(1)}, u32[]{:S(2)}, u32[]{:S(2)}) %collective-permute-start.10) | collective-permute-done | bytes 122912 | tf_op jit(solution)/shard_map/ppermute | solution.py:209
  32.3 0.0 collective-permute-start.11
  32.3 0.0 collective-permute-done.3.refs_4_
  32.3 0.5 %collective-permute-start.12 = (bf16[48,1280]{1,0:T(8,128)(2,1)S(1)}, bf16[48,1280]{1,0:T(8,128)(2,1)S(1)}, u32[]{:S(2)}, u32[]{:S(2)}) collective-permute-start(bf16[48,1280]{1,0:T(8,128)(2,1)S(1)} %collective-permute-done.8.refs_5_), channel_id=1, source_target_pairs={{0,1},{1,0},{2,3},{3,2},{4,5},{5,4},{6,7},{7,6},{8,9},{9,8},{10,11... | collective-permute-start | bytes 368648 | tf_op jit(solution)/shard_map/ppermute | solution.py:212
  32.8 0.0 collective-permute-done.4.refs_5_
  32.8 0.1 collective-permute-start.13
  32.9 0.0 collective-permute-done.5.refs_6_
  32.9 0.4 collective-permute-start.14
  33.3 0.0 collective-permute-done.6.refs_7_
  33.3 0.0 copy-start
  33.3 0.9 %copy-done = bf16[72,1280]{1,0:T(8,128)(2,1)S(1)} copy-done((bf16[72,1280]{1,0:T(8,128)(2,1)S(1)}, bf16[72,1280]{1,0:T(8,128)(2,1)}, u32[]{:S(2)}) %copy-start) | copy-done | bytes 184344
  34.2 0.7 %shard_map.56 = (f32[10,96,128]{2,1,0:T(8,128)S(1)}, f32[10,96,128]{2,1,0:T(8,128)S(1)}, f32[10,96,128]{2,1,0:T(8,128)S(1)}) custom-call(bf16[72,1280]{1,0:T(8,128)(2,1)S(1)} %copy-done, bf16[72,1280]{1,0:T(8,128)(2,1)S(1)} %collective-permute-done.refs_1_, bf16[72,1280]{1,0:T(8,128)(2,1)S(1)} %collective-permute-done.1.refs_2_, ...), custom_call_target="tpu_custom_call" | custom-call | tf_op jit(solution)/shard_map/pallas_call | solution.py:186
  35.0 0.0 collective-permute-done.11.refs_8_
  35.0 0.0 collective-permute-done.12.refs_9_
  35.0 0.0 collective-permute-done.13.refs_10_
  35.0 0.0 collective-permute-done.14.refs_11_
  35.0 1.0 %shard_map.57 = (bf16[24,1280]{1,0:T(8,128)(2,1)S(1)}, bf16[24,1280]{1,0:T(8,128)(2,1)S(1)}, bf16[24,1280]{1,0:T(8,128)(2,1)S(1)}, bf16[24,1280]{1,0:T(8,128)(2,1)S(1)}) custom-call(f32[10,96,128]{2,1,0:T(8,128)S(1)} %get-tuple-element.24.high_ref, f32[10,96,128]{2,1,0:T(8,128)S(1)} %get-tuple-element.25.sum_ref, ...), custom_call_target="tpu_custom_call" | custom-call | tf_op jit(solution)/shard_map/pallas_call | solution.py:186
  36.1 0.6 %collective-permute-start.15 = (bf16[24,1280]{1,0:T(8,128)(2,1)S(1)}, bf16[24,1280]{1,0:T(8,128)(2,1)S(1)}, u32[]{:S(2)}, u32[]{:S(2)}) collective-permute-start(bf16[24,1280]{1,0:T(8,128)(2,1)S(1)} %get-tuple-element.32), channel_id=1, source_target_pairs={{0,2},{2,0},{4,6},{6,4},{8,10},{10,8},{12,14},{14,12},{1,3},{3,1},... | collective-permute-start | bytes 184328 | tf_op jit(solution)/shard_map/ppermute | solution.py:209
  36.6 1.9 %collective-permute-start.16 = (bf16[24,1280]{1,0:T(8,128)(2,1)S(1)}, bf16[24,1280]{1,0:T(8,128)(2,1)S(1)}, u32[]{:S(2)}, u32[]{:S(2)}) collective-permute-start(bf16[24,1280]{1,0:T(8,128)(2,1)S(1)} %get-tuple-element.33), channel_id=1, source_target_pairs={{0,4},{2,6},{4,0},{6,2},{8,12},{10,14},{12,8},{14,10},{1,5},{3,7},... | collective-permute-start | bytes 184328 | tf_op jit(solution)/shard_map/ppermute | solution.py:209
  38.6 1.1 %collective-permute-start.17 = (bf16[24,1280]{1,0:T(8,128)(2,1)S(1)}, bf16[24,1280]{1,0:T(8,128)(2,1)S(1)}, u32[]{:S(2)}, u32[]{:S(2)}) collective-permute-start(bf16[24,1280]{1,0:T(8,128)(2,1)S(1)} %get-tuple-element.34), channel_id=1, source_target_pairs={{0,6},{2,4},{4,2},{6,0},{8,14},{10,12},{12,10},{14,8},{1,7},{3,5},... | collective-permute-start | bytes 184328 | tf_op jit(solution)/shard_map/ppermute | solution.py:209
  39.6 0.7 %collective-permute-done.15.refs_1_ = bf16[24,1280]{1,0:T(8,128)(2,1)S(1)} collective-permute-done((bf16[24,1280]{1,0:T(8,128)(2,1)S(1)}, bf16[24,1280]{1,0:T(8,128)(2,1)S(1)}, u32[]{:S(2)}, u32[]{:S(2)}) %collective-permute-start.15) | collective-permute-done | bytes 61472 | tf_op jit(solution)/shard_map/ppermute | solution.py:209
  40.4 0.5 %collective-permute-done.16.refs_2_ = bf16[24,1280]{1,0:T(8,128)(2,1)S(1)} collective-permute-done((bf16[24,1280]{1,0:T(8,128)(2,1)S(1)}, bf16[24,1280]{1,0:T(8,128)(2,1)S(1)}, u32[]{:S(2)}, u32[]{:S(2)}) %collective-permute-start.16) | collective-permute-done | bytes 61472 | tf_op jit(solution)/shard_map/ppermute | solution.py:209
  40.8 2.8 %collective-permute-done.17.refs_3_ = bf16[24,1280]{1,0:T(8,128)(2,1)S(1)} collective-permute-done((bf16[24,1280]{1,0:T(8,128)(2,1)S(1)}, bf16[24,1280]{1,0:T(8,128)(2,1)S(1)}, u32[]{:S(2)}, u32[]{:S(2)}) %collective-permute-start.17) | collective-permute-done | bytes 61472 | tf_op jit(solution)/shard_map/ppermute | solution.py:209
  43.7 0.7 %shard_map.58 = bf16[24,5120]{1,0:T(8,128)(2,1)} custom-call(s32[1]{0:T(128)} %bitcast.me_ref, bf16[24,1280]{1,0:T(8,128)(2,1)S(1)} %get-tuple-element.31.refs_0_, bf16[24,1280]{1,0:T(8,128)(2,1)S(1)} %collective-permute-done.15.refs_1_, bf16[24,1280]{1,0:T(8,128)(2,1)S(1)} %collective-permute-done.16.refs_2_, ...), custom_call_target="tpu_custom_call" | custom-call | tf_op jit(solution)/shard_map/pallas_call | solution.py:186
Async XLA Ops:
  2.5 10.8 %collective-permute-start.7 = (bf16[48,1280]{1,0:T(8,128)(2,1)}, bf16[48,1280]{1,0:T(8,128)(2,1)S(1)}, u32[]{:S(2)}, u32[]{:S(2)}) collective-permute-start(bf16[48,1280]{1,0:T(8,128)(2,1)} %get-tuple-element.27), channel_id=1, source_target_pairs={{0,8},{2,10},{4,12},{6,14},{8,0},{10,2},{12,4},{14,6},{1,9},{3,11}... | collective-permute-start | bytes 368648 | tf_op jit(solution)/shard_map/ppermute | solution.py:209
  6.6 16.4 %collective-permute-start = (bf16[72,1280]{1,0:T(8,128)(2,1)}, bf16[72,1280]{1,0:T(8,128)(2,1)S(1)}, u32[]{:S(2)}, u32[]{:S(2)}) collective-permute-start(bf16[72,1280]{1,0:T(8,128)(2,1)} %get-tuple-element.21), channel_id=1, source_target_pairs={{0,2},{2,0},{4,6},{6,4},{8,10},{10,8},{12,14},{14,12},{1,3},{3,1},... | collective-permute-start | bytes 552968 | tf_op jit(solution)/shard_map/ppermute | solution.py:209
  8.1 15.4 %collective-permute-start.1 = (bf16[72,1280]{1,0:T(8,128)(2,1)}, bf16[72,1280]{1,0:T(8,128)(2,1)S(1)}, u32[]{:S(2)}, u32[]{:S(2)}) collective-permute-start(bf16[72,1280]{1,0:T(8,128)(2,1)} %get-tuple-element.22), channel_id=1, source_target_pairs={{0,4},{2,6},{4,0},{6,2},{8,12},{10,14},{12,8},{14,10},{1,5},{3,7},... | collective-permute-start | bytes 552968 | tf_op jit(solution)/shard_map/ppermute | solution.py:209
  9.7 13.3 %collective-permute-start.8 = (bf16[48,1280]{1,0:T(8,128)(2,1)}, bf16[48,1280]{1,0:T(8,128)(2,1)S(1)}, u32[]{:S(2)}, u32[]{:S(2)}) collective-permute-start(bf16[48,1280]{1,0:T(8,128)(2,1)} %get-tuple-element.28), channel_id=1, source_target_pairs={{0,10},{2,8},{4,14},{6,12},{8,2},{10,0},{12,6},{14,4},{1,11},{3,9}... | collective-permute-start | bytes 368648 | tf_op jit(solution)/shard_map/ppermute | solution.py:209
  10.0 13.6 %collective-permute-start.9 = (bf16[48,1280]{1,0:T(8,128)(2,1)}, bf16[48,1280]{1,0:T(8,128)(2,1)S(1)}, u32[]{:S(2)}, u32[]{:S(2)}) collective-permute-start(bf16[48,1280]{1,0:T(8,128)(2,1)} %get-tuple-element.29), channel_id=1, source_target_pairs={{0,12},{2,14},{4,8},{6,10},{8,4},{10,6},{12,0},{14,2},{1,13},{3,15... | collective-permute-start | bytes 368648 | tf_op jit(solution)/shard_map/ppermute | solution.py:209
  13.3 12.4 %collective-permute-start.2 = (bf16[72,1280]{1,0:T(8,128)(2,1)}, bf16[72,1280]{1,0:T(8,128)(2,1)S(1)}, u32[]{:S(2)}, u32[]{:S(2)}) collective-permute-start(bf16[72,1280]{1,0:T(8,128)(2,1)} %get-tuple-element.23), channel_id=1, source_target_pairs={{0,6},{2,4},{4,2},{6,0},{8,14},{10,12},{12,10},{14,8},{1,7},{3,5},... | collective-permute-start | bytes 552968 | tf_op jit(solution)/shard_map/ppermute | solution.py:209
  23.0 9.3 %collective-permute-start.3 = (bf16[72,1280]{1,0:T(8,128)(2,1)}, bf16[72,1280]{1,0:T(8,128)(2,1)S(1)}, u32[]{:S(2)}, u32[]{:S(2)}) collective-permute-start(bf16[72,1280]{1,0:T(8,128)(2,1)} %get-tuple-element.20.refs_0_), channel_id=1, source_target_pairs={{0,1},{1,0},{2,3},{3,2},{4,5},{5,4},{6,7},{7,6},{8,9},{9,8},{10,11... | collective-permute-start | bytes 552968 | tf_op jit(solution)/shard_map/ppermute | solution.py:212
  23.0 9.8 %collective-permute-start.4 = (bf16[72,1280]{1,0:T(8,128)(2,1)S(1)}, bf16[72,1280]{1,0:T(8,128)(2,1)S(1)}, u32[]{:S(2)}, u32[]{:S(2)}) collective-permute-start(bf16[72,1280]{1,0:T(8,128)(2,1)S(1)} %collective-permute-done.refs_1_), channel_id=1, source_target_pairs={{0,1},{1,0},{2,3},{3,2},{4,5},{5,4},{6,7},{7,6},{8,9},{9,8},{10,11... | collective-permute-start | bytes 552968 | tf_op jit(solution)/shard_map/ppermute | solution.py:212
  23.5 9.3 %collective-permute-start.5 = (bf16[72,1280]{1,0:T(8,128)(2,1)S(1)}, bf16[72,1280]{1,0:T(8,128)(2,1)S(1)}, u32[]{:S(2)}, u32[]{:S(2)}) collective-permute-start(bf16[72,1280]{1,0:T(8,128)(2,1)S(1)} %collective-permute-done.1.refs_2_), channel_id=1, source_target_pairs={{0,1},{1,0},{2,3},{3,2},{4,5},{5,4},{6,7},{7,6},{8,9},{9,8},{10,11... | collective-permute-start | bytes 552968 | tf_op jit(solution)/shard_map/ppermute | solution.py:212
  23.6 8.7 %collective-permute-start.10 = (bf16[48,1280]{1,0:T(8,128)(2,1)}, bf16[48,1280]{1,0:T(8,128)(2,1)S(1)}, u32[]{:S(2)}, u32[]{:S(2)}) collective-permute-start(bf16[48,1280]{1,0:T(8,128)(2,1)} %get-tuple-element.30), channel_id=1, source_target_pairs={{0,14},{2,12},{4,10},{6,8},{8,6},{10,4},{12,2},{14,0},{1,15},{3,13... | collective-permute-start | bytes 368648 | tf_op jit(solution)/shard_map/ppermute | solution.py:209
  25.7 7.6 %collective-permute-start.6 = (bf16[72,1280]{1,0:T(8,128)(2,1)S(1)}, bf16[72,1280]{1,0:T(8,128)(2,1)S(1)}, u32[]{:S(2)}, u32[]{:S(2)}) collective-permute-start(bf16[72,1280]{1,0:T(8,128)(2,1)S(1)} %collective-permute-done.2.refs_3_), channel_id=1, source_target_pairs={{0,1},{1,0},{2,3},{3,2},{4,5},{5,4},{6,7},{7,6},{8,9},{9,8},{10,11... | collective-permute-start | bytes 552968 | tf_op jit(solution)/shard_map/ppermute | solution.py:212
  32.3 2.7 %collective-permute-start.11 = (bf16[48,1280]{1,0:T(8,128)(2,1)S(1)}, bf16[48,1280]{1,0:T(8,128)(2,1)S(1)}, u32[]{:S(2)}, u32[]{:S(2)}) collective-permute-start(bf16[48,1280]{1,0:T(8,128)(2,1)S(1)} %collective-permute-done.7.refs_4_), channel_id=1, source_target_pairs={{0,1},{1,0},{2,3},{3,2},{4,5},{5,4},{6,7},{7,6},{8,9},{9,8},{10,11... | collective-permute-start | bytes 368648 | tf_op jit(solution)/shard_map/ppermute | solution.py:212
  32.3 2.7 %collective-permute-start.12 = (bf16[48,1280]{1,0:T(8,128)(2,1)S(1)}, bf16[48,1280]{1,0:T(8,128)(2,1)S(1)}, u32[]{:S(2)}, u32[]{:S(2)}) collective-permute-start(bf16[48,1280]{1,0:T(8,128)(2,1)S(1)} %collective-permute-done.8.refs_5_), channel_id=1, source_target_pairs={{0,1},{1,0},{2,3},{3,2},{4,5},{5,4},{6,7},{7,6},{8,9},{9,8},{10,11... | collective-permute-start | bytes 368648 | tf_op jit(solution)/shard_map/ppermute | solution.py:212
  32.8 2.2 %collective-permute-start.13 = (bf16[48,1280]{1,0:T(8,128)(2,1)S(1)}, bf16[48,1280]{1,0:T(8,128)(2,1)S(1)}, u32[]{:S(2)}, u32[]{:S(2)}) collective-permute-start(bf16[48,1280]{1,0:T(8,128)(2,1)S(1)} %collective-permute-done.9.refs_6_), channel_id=1, source_target_pairs={{0,1},{1,0},{2,3},{3,2},{4,5},{5,4},{6,7},{7,6},{8,9},{9,8},{10,11... | collective-permute-start | bytes 368648 | tf_op jit(solution)/shard_map/ppermute | solution.py:212
  32.9 2.2 %collective-permute-start.14 = (bf16[48,1280]{1,0:T(8,128)(2,1)S(1)}, bf16[48,1280]{1,0:T(8,128)(2,1)S(1)}, u32[]{:S(2)}, u32[]{:S(2)}) collective-permute-start(bf16[48,1280]{1,0:T(8,128)(2,1)S(1)} %collective-permute-done.10.refs_7_), channel_id=1, source_target_pairs={{0,1},{1,0},{2,3},{3,2},{4,5},{5,4},{6,7},{7,6},{8,9},{9,8},{10,11... | collective-permute-start | bytes 368648 | tf_op jit(solution)/shard_map/ppermute | solution.py:212
  33.3 0.9 %copy-start = (bf16[72,1280]{1,0:T(8,128)(2,1)S(1)}, bf16[72,1280]{1,0:T(8,128)(2,1)}, u32[]{:S(2)}) copy-start(bf16[72,1280]{1,0:T(8,128)(2,1)} %get-tuple-element.20.refs_0_) | copy-start | bytes 552964
  36.1 4.3 %collective-permute-start.15 = (bf16[24,1280]{1,0:T(8,128)(2,1)S(1)}, bf16[24,1280]{1,0:T(8,128)(2,1)S(1)}, u32[]{:S(2)}, u32[]{:S(2)}) collective-permute-start(bf16[24,1280]{1,0:T(8,128)(2,1)S(1)} %get-tuple-element.32), channel_id=1, source_target_pairs={{0,2},{2,0},{4,6},{6,4},{8,10},{10,8},{12,14},{14,12},{1,3},{3,1},... | collective-permute-start | bytes 184328 | tf_op jit(solution)/shard_map/ppermute | solution.py:209
  36.6 4.2 %collective-permute-start.16 = (bf16[24,1280]{1,0:T(8,128)(2,1)S(1)}, bf16[24,1280]{1,0:T(8,128)(2,1)S(1)}, u32[]{:S(2)}, u32[]{:S(2)}) collective-permute-start(bf16[24,1280]{1,0:T(8,128)(2,1)S(1)} %get-tuple-element.33), channel_id=1, source_target_pairs={{0,4},{2,6},{4,0},{6,2},{8,12},{10,14},{12,8},{14,10},{1,5},{3,7},... | collective-permute-start | bytes 184328 | tf_op jit(solution)/shard_map/ppermute | solution.py:209
  38.6 5.1 %collective-permute-start.17 = (bf16[24,1280]{1,0:T(8,128)(2,1)S(1)}, bf16[24,1280]{1,0:T(8,128)(2,1)S(1)}, u32[]{:S(2)}, u32[]{:S(2)}) collective-permute-start(bf16[24,1280]{1,0:T(8,128)(2,1)S(1)} %get-tuple-element.34), channel_id=1, source_target_pairs={{0,6},{2,4},{4,2},{6,0},{8,14},{10,12},{12,10},{14,8},{1,7},{3,5},... | collective-permute-start | bytes 184328 | tf_op jit(solution)/shard_map/ppermute | solution.py:209

commit v3 on v2

--- a/solution.py
+++ b/solution.py
@@ -216,14 +216,17 @@
     far = jax.ShapeDtypeStruct((2 * rows, part), BF16)
     token = pltpu.VMEM((rows, width), BF16)
     gain = pltpu.VMEM((1, width), F32)
+    held = [
+        pltpu.with_memory_space_constraint(value, pltpu.HBM)
+        for value in (queries, keys, values, q_gain[None, :], k_gain[None, :])
+    ]
     packed = kernel_call(
         functools.partial(pack_kernel, groups),
         [full] * groups + [far] * groups,
         scalars=1,
         fetched=range(1, 6),
-        limit=60 << 20,
         scratch=[token] * 3 + [gain] * 2 + [pltpu.SemaphoreType.DMA((5,))],
-    )(me, queries, keys, values, q_gain[None, :], k_gain[None, :])
+    )(me, *held)
     fulls, fars = packed[:groups], packed[groups:]
     far_in = [send(fars[step], 1, step) for step in steps]
     near_in = [fulls[0]] + [send(fulls[step], 0, step) for step in steps[1:]]

time: 44.5 us -> 42.3 us (0.951)
  Pallas kernels: 4.95 us -> 3.99 us
  local copies, waits for them, and re-layouts: 0.92 us -> 0 us
    pallas_call x4, Pallas kernels: 4.95 us -> 3.99 us  [call(): pl.pallas_call(kernel, out_shape=shapes, in_specs=places, out_specs=jax.t...]
    unnamed x2 -> x0, local copies, waits for them, and re-layouts: 0.92 us -> none
  transfers between devices with their start and end apart: 18 -> 18, of which waited for: 6 -> 7; matrix products, arithmetic and copies ran while one was open for 0% -> 0% of each run, Pallas kernels for 2% -> 2%
where the time goes in v3:
time: 42.3 us; the launch traced here: 42.2 us
  waiting for transfers between devices  19.5 us (46%)
  starting transfers between devices  18.6 us (44%)
  Pallas kernels  3.99 us (9%)
    ppermute x10, waiting for transfers between devices, send(): lax.ppermute(value, CHIP, [(i, i ^ place) for i in range(seq * across)])  19.3 us
    ppermute x10, starting transfers between devices, send(): lax.ppermute(value, CHIP, [(i, i ^ place) for i in range(seq * across)])  16.9 us
    pallas_call x4, Pallas kernels, call(): pl.pallas_call(kernel, out_shape=shapes, in_specs=places, out_specs=jax.t...  3.99 us
    ppermute x8, starting transfers between devices, swap(): return lax.ppermute(value, 'sub', SWAP)  1.76 us
  transfers between devices with their start and end apart: 18, of which 7 were waited for; matrix products, arithmetic and copies ran while one was open for 0% of the time, Pallas kernels for 2%

profile of v3, /device:TPU:0, one launch (start us, length us, event | category | flops | bytes accessed | tf_op | source)
XLA Modules:
  0.0 42.2 jit_solution(5564624131902037868)
XLA Ops:
  0.0 1.5 %shard_map.55 = (bf16[72,1280]{1,0:T(8,128)(2,1)S(1)}, bf16[72,1280]{1,0:T(8,128)(2,1)S(1)}, bf16[72,1280]{1,0:T(8,128)(2,1)S(1)}, bf16[72,1280]{1,0:T(8,128)(2,...) custom-call(s32[1]{0:T(128)} %bitcast.me_ref, ...), custom_call_target="tpu_custom_call" | custom-call | tf_op jit(solution)/shard_map/pallas_call | solution.py:186
  1.5 4.1 %collective-permute-start.7 = (bf16[48,1280]{1,0:T(8,128)(2,1)S(1)}, bf16[48,1280]{1,0:T(8,128)(2,1)S(1)}, u32[]{:S(2)}, u32[]{:S(2)}) collective-permute-start(bf16[48,1280]{1,0:T(8,128)(2,1)S(1)} %get-tuple-element.27), channel_id=1, source_target_pairs={{0,8},{2,10},{4,12},{6,14},{8,0},{10,2},{12,4},{14,6},{1,9},{3,11}... | collective-permute-start | bytes 368648 | tf_op jit(solution)/shard_map/ppermute | solution.py:209
  5.6 1.5 %collective-permute-start = (bf16[72,1280]{1,0:T(8,128)(2,1)S(1)}, bf16[72,1280]{1,0:T(8,128)(2,1)S(1)}, u32[]{:S(2)}, u32[]{:S(2)}) collective-permute-start(bf16[72,1280]{1,0:T(8,128)(2,1)S(1)} %get-tuple-element.21), channel_id=1, source_target_pairs={{0,2},{2,0},{4,6},{6,4},{8,10},{10,8},{12,14},{14,12},{1,3},{3,1},... | collective-permute-start | bytes 552968 | tf_op jit(solution)/shard_map/ppermute | solution.py:209
  7.1 1.6 %collective-permute-start.1 = (bf16[72,1280]{1,0:T(8,128)(2,1)S(1)}, bf16[72,1280]{1,0:T(8,128)(2,1)S(1)}, u32[]{:S(2)}, u32[]{:S(2)}) collective-permute-start(bf16[72,1280]{1,0:T(8,128)(2,1)S(1)} %get-tuple-element.22), channel_id=1, source_target_pairs={{0,4},{2,6},{4,0},{6,2},{8,12},{10,14},{12,8},{14,10},{1,5},{3,7},... | collective-permute-start | bytes 552968 | tf_op jit(solution)/shard_map/ppermute | solution.py:209
  8.7 0.3 collective-permute-start.8
  9.0 2.5 %collective-permute-start.9 = (bf16[48,1280]{1,0:T(8,128)(2,1)S(1)}, bf16[48,1280]{1,0:T(8,128)(2,1)S(1)}, u32[]{:S(2)}, u32[]{:S(2)}) collective-permute-start(bf16[48,1280]{1,0:T(8,128)(2,1)S(1)} %get-tuple-element.29), channel_id=1, source_target_pairs={{0,12},{2,14},{4,8},{6,10},{8,4},{10,6},{12,0},{14,2},{1,13},{3,15... | collective-permute-start | bytes 368648 | tf_op jit(solution)/shard_map/ppermute | solution.py:209
  11.5 0.6 %collective-permute-done.7.refs_4_ = bf16[48,1280]{1,0:T(8,128)(2,1)S(1)} collective-permute-done((bf16[48,1280]{1,0:T(8,128)(2,1)S(1)}, bf16[48,1280]{1,0:T(8,128)(2,1)S(1)}, u32[]{:S(2)}, u32[]{:S(2)}) %collective-permute-start.7) | collective-permute-done | bytes 122912 | tf_op jit(solution)/shard_map/ppermute | solution.py:209
  12.1 1.3 %collective-permute-start.2 = (bf16[72,1280]{1,0:T(8,128)(2,1)S(1)}, bf16[72,1280]{1,0:T(8,128)(2,1)S(1)}, u32[]{:S(2)}, u32[]{:S(2)}) collective-permute-start(bf16[72,1280]{1,0:T(8,128)(2,1)S(1)} %get-tuple-element.23), channel_id=1, source_target_pairs={{0,6},{2,4},{4,2},{6,0},{8,14},{10,12},{12,10},{14,8},{1,7},{3,5},... | collective-permute-start | bytes 552968 | tf_op jit(solution)/shard_map/ppermute | solution.py:209
  13.4 8.4 %collective-permute-done.8.refs_5_ = bf16[48,1280]{1,0:T(8,128)(2,1)S(1)} collective-permute-done((bf16[48,1280]{1,0:T(8,128)(2,1)S(1)}, bf16[48,1280]{1,0:T(8,128)(2,1)S(1)}, u32[]{:S(2)}, u32[]{:S(2)}) %collective-permute-start.8) | collective-permute-done | bytes 122912 | tf_op jit(solution)/shard_map/ppermute | solution.py:209
  21.8 0.0 collective-permute-start.3
  21.8 0.0 collective-permute-done.refs_1_
  21.8 0.5 %collective-permute-start.4 = (bf16[72,1280]{1,0:T(8,128)(2,1)S(1)}, bf16[72,1280]{1,0:T(8,128)(2,1)S(1)}, u32[]{:S(2)}, u32[]{:S(2)}) collective-permute-start(bf16[72,1280]{1,0:T(8,128)(2,1)S(1)} %collective-permute-done.refs_1_), channel_id=1, source_target_pairs={{0,1},{1,0},{2,3},{3,2},{4,5},{5,4},{6,7},{7,6},{8,9},{9,8},{10,11... | collective-permute-start | bytes 552968 | tf_op jit(solution)/shard_map/ppermute | solution.py:212
  22.3 0.0 collective-permute-done.1.refs_2_
  22.3 0.1 collective-permute-start.5
  22.4 0.0 collective-permute-done.9.refs_6_
  22.4 2.1 %collective-permute-start.10 = (bf16[48,1280]{1,0:T(8,128)(2,1)S(1)}, bf16[48,1280]{1,0:T(8,128)(2,1)S(1)}, u32[]{:S(2)}, u32[]{:S(2)}) collective-permute-start(bf16[48,1280]{1,0:T(8,128)(2,1)S(1)} %get-tuple-element.30), channel_id=1, source_target_pairs={{0,14},{2,12},{4,10},{6,8},{8,6},{10,4},{12,2},{14,0},{1,15},{3,13... | collective-permute-start | bytes 368648 | tf_op jit(solution)/shard_map/ppermute | solution.py:209
  24.5 0.0 collective-permute-done.2.refs_3_
  24.5 0.2 collective-permute-start.6
  24.7 6.2 %collective-permute-done.10.refs_7_ = bf16[48,1280]{1,0:T(8,128)(2,1)S(1)} collective-permute-done((bf16[48,1280]{1,0:T(8,128)(2,1)S(1)}, bf16[48,1280]{1,0:T(8,128)(2,1)S(1)}, u32[]{:S(2)}, u32[]{:S(2)}) %collective-permute-start.10) | collective-permute-done | bytes 122912 | tf_op jit(solution)/shard_map/ppermute | solution.py:209
  30.9 0.0 collective-permute-start.11
  30.9 0.0 collective-permute-done.3.refs_4_
  30.9 0.5 %collective-permute-start.12 = (bf16[48,1280]{1,0:T(8,128)(2,1)S(1)}, bf16[48,1280]{1,0:T(8,128)(2,1)S(1)}, u32[]{:S(2)}, u32[]{:S(2)}) collective-permute-start(bf16[48,1280]{1,0:T(8,128)(2,1)S(1)} %collective-permute-done.8.refs_5_), channel_id=1, source_target_pairs={{0,1},{1,0},{2,3},{3,2},{4,5},{5,4},{6,7},{7,6},{8,9},{9,8},{10,11... | collective-permute-start | bytes 368648 | tf_op jit(solution)/shard_map/ppermute | solution.py:212
  31.4 0.0 collective-permute-done.4.refs_5_
  31.4 0.1 collective-permute-start.13
  31.5 0.0 collective-permute-done.5.refs_6_
  31.5 0.4 %collective-permute-start.14 = (bf16[48,1280]{1,0:T(8,128)(2,1)S(1)}, bf16[48,1280]{1,0:T(8,128)(2,1)S(1)}, u32[]{:S(2)}, u32[]{:S(2)}) collective-permute-start(bf16[48,1280]{1,0:T(8,128)(2,1)S(1)} %collective-permute-done.10.refs_7_), channel_id=1, source_target_pairs={{0,1},{1,0},{2,3},{3,2},{4,5},{5,4},{6,7},{7,6},{8,9},{9,8},{10,11... | collective-permute-start | bytes 368648 | tf_op jit(solution)/shard_map/ppermute | solution.py:212
  31.9 0.0 collective-permute-done.6.refs_7_
  31.9 0.7 %shard_map.56 = (f32[10,96,128]{2,1,0:T(8,128)S(1)}, f32[10,96,128]{2,1,0:T(8,128)S(1)}, f32[10,96,128]{2,1,0:T(8,128)S(1)}) custom-call(bf16[72,1280]{1,0:T(8,128)(2,1)S(1)} %get-tuple-element.20.refs_0_, bf16[72,1280]{1,0:T(8,128)(2,1)S(1)} %collective-permute-done.refs_1_, bf16[72,1280]{1,0:T(8,128)(2,1)S(1)} %collective-permute-done.1.refs_2_, ...), custom_call_target="tpu_custom_call" | custom-call | tf_op jit(solution)/shard_map/pallas_call | solution.py:186
  32.7 0.0 collective-permute-done.11.refs_8_
  32.7 0.0 collective-permute-done.12.refs_9_
  32.7 0.0 collective-permute-done.13.refs_10_
  32.7 0.2 collective-permute-done.14.refs_11_
  32.9 1.0 %shard_map.57 = (bf16[24,1280]{1,0:T(8,128)(2,1)S(1)}, bf16[24,1280]{1,0:T(8,128)(2,1)S(1)}, bf16[24,1280]{1,0:T(8,128)(2,1)S(1)}, bf16[24,1280]{1,0:T(8,128)(2,1)S(1)}) custom-call(f32[10,96,128]{2,1,0:T(8,128)S(1)} %get-tuple-element.24.high_ref, f32[10,96,128]{2,1,0:T(8,128)S(1)} %get-tuple-element.25.sum_ref, ...), custom_call_target="tpu_custom_call" | custom-call | tf_op jit(solution)/shard_map/pallas_call | solution.py:186
  34.0 0.6 %collective-permute-start.15 = (bf16[24,1280]{1,0:T(8,128)(2,1)S(1)}, bf16[24,1280]{1,0:T(8,128)(2,1)S(1)}, u32[]{:S(2)}, u32[]{:S(2)}) collective-permute-start(bf16[24,1280]{1,0:T(8,128)(2,1)S(1)} %get-tuple-element.32), channel_id=1, source_target_pairs={{0,2},{2,0},{4,6},{6,4},{8,10},{10,8},{12,14},{14,12},{1,3},{3,1},... | collective-permute-start | bytes 184328 | tf_op jit(solution)/shard_map/ppermute | solution.py:209
  34.5 1.8 %collective-permute-start.16 = (bf16[24,1280]{1,0:T(8,128)(2,1)S(1)}, bf16[24,1280]{1,0:T(8,128)(2,1)S(1)}, u32[]{:S(2)}, u32[]{:S(2)}) collective-permute-start(bf16[24,1280]{1,0:T(8,128)(2,1)S(1)} %get-tuple-element.33), channel_id=1, source_target_pairs={{0,4},{2,6},{4,0},{6,2},{8,12},{10,14},{12,8},{14,10},{1,5},{3,7},... | collective-permute-start | bytes 184328 | tf_op jit(solution)/shard_map/ppermute | solution.py:209
  36.3 1.2 %collective-permute-start.17 = (bf16[24,1280]{1,0:T(8,128)(2,1)S(1)}, bf16[24,1280]{1,0:T(8,128)(2,1)S(1)}, u32[]{:S(2)}, u32[]{:S(2)}) collective-permute-start(bf16[24,1280]{1,0:T(8,128)(2,1)S(1)} %get-tuple-element.34), channel_id=1, source_target_pairs={{0,6},{2,4},{4,2},{6,0},{8,14},{10,12},{12,10},{14,8},{1,7},{3,5},... | collective-permute-start | bytes 184328 | tf_op jit(solution)/shard_map/ppermute | solution.py:209
  37.5 0.8 %collective-permute-done.15.refs_1_ = bf16[24,1280]{1,0:T(8,128)(2,1)S(1)} collective-permute-done((bf16[24,1280]{1,0:T(8,128)(2,1)S(1)}, bf16[24,1280]{1,0:T(8,128)(2,1)S(1)}, u32[]{:S(2)}, u32[]{:S(2)}) %collective-permute-start.15) | collective-permute-done | bytes 61472 | tf_op jit(solution)/shard_map/ppermute | solution.py:209
  38.3 0.5 %collective-permute-done.16.refs_2_ = bf16[24,1280]{1,0:T(8,128)(2,1)S(1)} collective-permute-done((bf16[24,1280]{1,0:T(8,128)(2,1)S(1)}, bf16[24,1280]{1,0:T(8,128)(2,1)S(1)}, u32[]{:S(2)}, u32[]{:S(2)}) %collective-permute-start.16) | collective-permute-done | bytes 61472 | tf_op jit(solution)/shard_map/ppermute | solution.py:209
  38.7 2.7 %collective-permute-done.17.refs_3_ = bf16[24,1280]{1,0:T(8,128)(2,1)S(1)} collective-permute-done((bf16[24,1280]{1,0:T(8,128)(2,1)S(1)}, bf16[24,1280]{1,0:T(8,128)(2,1)S(1)}, u32[]{:S(2)}, u32[]{:S(2)}) %collective-permute-start.17) | collective-permute-done | bytes 61472 | tf_op jit(solution)/shard_map/ppermute | solution.py:209
  41.5 0.7 %shard_map.58 = bf16[24,5120]{1,0:T(8,128)(2,1)} custom-call(s32[1]{0:T(128)} %bitcast.me_ref, bf16[24,1280]{1,0:T(8,128)(2,1)S(1)} %get-tuple-element.31.refs_0_, bf16[24,1280]{1,0:T(8,128)(2,1)S(1)} %collective-permute-done.15.refs_1_, bf16[24,1280]{1,0:T(8,128)(2,1)S(1)} %collective-permute-done.16.refs_2_, ...), custom_call_target="tpu_custom_call" | custom-call | tf_op jit(solution)/shard_map/pallas_call | solution.py:186
Async XLA Ops:
  1.5 10.6 %collective-permute-start.7 = (bf16[48,1280]{1,0:T(8,128)(2,1)S(1)}, bf16[48,1280]{1,0:T(8,128)(2,1)S(1)}, u32[]{:S(2)}, u32[]{:S(2)}) collective-permute-start(bf16[48,1280]{1,0:T(8,128)(2,1)S(1)} %get-tuple-element.27), channel_id=1, source_target_pairs={{0,8},{2,10},{4,12},{6,14},{8,0},{10,2},{12,4},{14,6},{1,9},{3,11}... | collective-permute-start | bytes 368648 | tf_op jit(solution)/shard_map/ppermute | solution.py:209
  5.6 16.2 %collective-permute-start = (bf16[72,1280]{1,0:T(8,128)(2,1)S(1)}, bf16[72,1280]{1,0:T(8,128)(2,1)S(1)}, u32[]{:S(2)}, u32[]{:S(2)}) collective-permute-start(bf16[72,1280]{1,0:T(8,128)(2,1)S(1)} %get-tuple-element.21), channel_id=1, source_target_pairs={{0,2},{2,0},{4,6},{6,4},{8,10},{10,8},{12,14},{14,12},{1,3},{3,1},... | collective-permute-start | bytes 552968 | tf_op jit(solution)/shard_map/ppermute | solution.py:209
  7.1 15.2 %collective-permute-start.1 = (bf16[72,1280]{1,0:T(8,128)(2,1)S(1)}, bf16[72,1280]{1,0:T(8,128)(2,1)S(1)}, u32[]{:S(2)}, u32[]{:S(2)}) collective-permute-start(bf16[72,1280]{1,0:T(8,128)(2,1)S(1)} %get-tuple-element.22), channel_id=1, source_target_pairs={{0,4},{2,6},{4,0},{6,2},{8,12},{10,14},{12,8},{14,10},{1,5},{3,7},... | collective-permute-start | bytes 552968 | tf_op jit(solution)/shard_map/ppermute | solution.py:209
  8.7 13.1 %collective-permute-start.8 = (bf16[48,1280]{1,0:T(8,128)(2,1)S(1)}, bf16[48,1280]{1,0:T(8,128)(2,1)S(1)}, u32[]{:S(2)}, u32[]{:S(2)}) collective-permute-start(bf16[48,1280]{1,0:T(8,128)(2,1)S(1)} %get-tuple-element.28), channel_id=1, source_target_pairs={{0,10},{2,8},{4,14},{6,12},{8,2},{10,0},{12,6},{14,4},{1,11},{3,9}... | collective-permute-start | bytes 368648 | tf_op jit(solution)/shard_map/ppermute | solution.py:209
  9.0 13.4 %collective-permute-start.9 = (bf16[48,1280]{1,0:T(8,128)(2,1)S(1)}, bf16[48,1280]{1,0:T(8,128)(2,1)S(1)}, u32[]{:S(2)}, u32[]{:S(2)}) collective-permute-start(bf16[48,1280]{1,0:T(8,128)(2,1)S(1)} %get-tuple-element.29), channel_id=1, source_target_pairs={{0,12},{2,14},{4,8},{6,10},{8,4},{10,6},{12,0},{14,2},{1,13},{3,15... | collective-permute-start | bytes 368648 | tf_op jit(solution)/shard_map/ppermute | solution.py:209
  12.1 12.4 %collective-permute-start.2 = (bf16[72,1280]{1,0:T(8,128)(2,1)S(1)}, bf16[72,1280]{1,0:T(8,128)(2,1)S(1)}, u32[]{:S(2)}, u32[]{:S(2)}) collective-permute-start(bf16[72,1280]{1,0:T(8,128)(2,1)S(1)} %get-tuple-element.23), channel_id=1, source_target_pairs={{0,6},{2,4},{4,2},{6,0},{8,14},{10,12},{12,10},{14,8},{1,7},{3,5},... | collective-permute-start | bytes 552968 | tf_op jit(solution)/shard_map/ppermute | solution.py:209
  21.8 9.1 %collective-permute-start.3 = (bf16[72,1280]{1,0:T(8,128)(2,1)S(1)}, bf16[72,1280]{1,0:T(8,128)(2,1)S(1)}, u32[]{:S(2)}, u32[]{:S(2)}) collective-permute-start(bf16[72,1280]{1,0:T(8,128)(2,1)S(1)} %get-tuple-element.20.refs_0_), channel_id=1, source_target_pairs={{0,1},{1,0},{2,3},{3,2},{4,5},{5,4},{6,7},{7,6},{8,9},{9,8},{10,11... | collective-permute-start | bytes 552968 | tf_op jit(solution)/shard_map/ppermute | solution.py:212
  21.8 9.6 %collective-permute-start.4 = (bf16[72,1280]{1,0:T(8,128)(2,1)S(1)}, bf16[72,1280]{1,0:T(8,128)(2,1)S(1)}, u32[]{:S(2)}, u32[]{:S(2)}) collective-permute-start(bf16[72,1280]{1,0:T(8,128)(2,1)S(1)} %collective-permute-done.refs_1_), channel_id=1, source_target_pairs={{0,1},{1,0},{2,3},{3,2},{4,5},{5,4},{6,7},{7,6},{8,9},{9,8},{10,11... | collective-permute-start | bytes 552968 | tf_op jit(solution)/shard_map/ppermute | solution.py:212
  22.3 9.1 %collective-permute-start.5 = (bf16[72,1280]{1,0:T(8,128)(2,1)S(1)}, bf16[72,1280]{1,0:T(8,128)(2,1)S(1)}, u32[]{:S(2)}, u32[]{:S(2)}) collective-permute-start(bf16[72,1280]{1,0:T(8,128)(2,1)S(1)} %collective-permute-done.1.refs_2_), channel_id=1, source_target_pairs={{0,1},{1,0},{2,3},{3,2},{4,5},{5,4},{6,7},{7,6},{8,9},{9,8},{10,11... | collective-permute-start | bytes 552968 | tf_op jit(solution)/shard_map/ppermute | solution.py:212
  22.4 8.5 %collective-permute-start.10 = (bf16[48,1280]{1,0:T(8,128)(2,1)S(1)}, bf16[48,1280]{1,0:T(8,128)(2,1)S(1)}, u32[]{:S(2)}, u32[]{:S(2)}) collective-permute-start(bf16[48,1280]{1,0:T(8,128)(2,1)S(1)} %get-tuple-element.30), channel_id=1, source_target_pairs={{0,14},{2,12},{4,10},{6,8},{8,6},{10,4},{12,2},{14,0},{1,15},{3,13... | collective-permute-start | bytes 368648 | tf_op jit(solution)/shard_map/ppermute | solution.py:209
  24.5 7.4 %collective-permute-start.6 = (bf16[72,1280]{1,0:T(8,128)(2,1)S(1)}, bf16[72,1280]{1,0:T(8,128)(2,1)S(1)}, u32[]{:S(2)}, u32[]{:S(2)}) collective-permute-start(bf16[72,1280]{1,0:T(8,128)(2,1)S(1)} %collective-permute-done.2.refs_3_), channel_id=1, source_target_pairs={{0,1},{1,0},{2,3},{3,2},{4,5},{5,4},{6,7},{7,6},{8,9},{9,8},{10,11... | collective-permute-start | bytes 552968 | tf_op jit(solution)/shard_map/ppermute | solution.py:212
  30.9 1.8 %collective-permute-start.11 = (bf16[48,1280]{1,0:T(8,128)(2,1)S(1)}, bf16[48,1280]{1,0:T(8,128)(2,1)S(1)}, u32[]{:S(2)}, u32[]{:S(2)}) collective-permute-start(bf16[48,1280]{1,0:T(8,128)(2,1)S(1)} %collective-permute-done.7.refs_4_), channel_id=1, source_target_pairs={{0,1},{1,0},{2,3},{3,2},{4,5},{5,4},{6,7},{7,6},{8,9},{9,8},{10,11... | collective-permute-start | bytes 368648 | tf_op jit(solution)/shard_map/ppermute | solution.py:212
  30.9 1.8 %collective-permute-start.12 = (bf16[48,1280]{1,0:T(8,128)(2,1)S(1)}, bf16[48,1280]{1,0:T(8,128)(2,1)S(1)}, u32[]{:S(2)}, u32[]{:S(2)}) collective-permute-start(bf16[48,1280]{1,0:T(8,128)(2,1)S(1)} %collective-permute-done.8.refs_5_), channel_id=1, source_target_pairs={{0,1},{1,0},{2,3},{3,2},{4,5},{5,4},{6,7},{7,6},{8,9},{9,8},{10,11... | collective-permute-start | bytes 368648 | tf_op jit(solution)/shard_map/ppermute | solution.py:212
  31.4 1.3 %collective-permute-start.13 = (bf16[48,1280]{1,0:T(8,128)(2,1)S(1)}, bf16[48,1280]{1,0:T(8,128)(2,1)S(1)}, u32[]{:S(2)}, u32[]{:S(2)}) collective-permute-start(bf16[48,1280]{1,0:T(8,128)(2,1)S(1)} %collective-permute-done.9.refs_6_), channel_id=1, source_target_pairs={{0,1},{1,0},{2,3},{3,2},{4,5},{5,4},{6,7},{7,6},{8,9},{9,8},{10,11... | collective-permute-start | bytes 368648 | tf_op jit(solution)/shard_map/ppermute | solution.py:212
  31.5 1.4 %collective-permute-start.14 = (bf16[48,1280]{1,0:T(8,128)(2,1)S(1)}, bf16[48,1280]{1,0:T(8,128)(2,1)S(1)}, u32[]{:S(2)}, u32[]{:S(2)}) collective-permute-start(bf16[48,1280]{1,0:T(8,128)(2,1)S(1)} %collective-permute-done.10.refs_7_), channel_id=1, source_target_pairs={{0,1},{1,0},{2,3},{3,2},{4,5},{5,4},{6,7},{7,6},{8,9},{9,8},{10,11... | collective-permute-start | bytes 368648 | tf_op jit(solution)/shard_map/ppermute | solution.py:212
  34.0 4.3 %collective-permute-start.15 = (bf16[24,1280]{1,0:T(8,128)(2,1)S(1)}, bf16[24,1280]{1,0:T(8,128)(2,1)S(1)}, u32[]{:S(2)}, u32[]{:S(2)}) collective-permute-start(bf16[24,1280]{1,0:T(8,128)(2,1)S(1)} %get-tuple-element.32), channel_id=1, source_target_pairs={{0,2},{2,0},{4,6},{6,4},{8,10},{10,8},{12,14},{14,12},{1,3},{3,1},... | collective-permute-start | bytes 184328 | tf_op jit(solution)/shard_map/ppermute | solution.py:209
  34.5 4.2 %collective-permute-start.16 = (bf16[24,1280]{1,0:T(8,128)(2,1)S(1)}, bf16[24,1280]{1,0:T(8,128)(2,1)S(1)}, u32[]{:S(2)}, u32[]{:S(2)}) collective-permute-start(bf16[24,1280]{1,0:T(8,128)(2,1)S(1)} %get-tuple-element.33), channel_id=1, source_target_pairs={{0,4},{2,6},{4,0},{6,2},{8,12},{10,14},{12,8},{14,10},{1,5},{3,7},... | collective-permute-start | bytes 184328 | tf_op jit(solution)/shard_map/ppermute | solution.py:209
  36.3 5.1 %collective-permute-start.17 = (bf16[24,1280]{1,0:T(8,128)(2,1)S(1)}, bf16[24,1280]{1,0:T(8,128)(2,1)S(1)}, u32[]{:S(2)}, u32[]{:S(2)}) collective-permute-start(bf16[24,1280]{1,0:T(8,128)(2,1)S(1)} %get-tuple-element.34), channel_id=1, source_target_pairs={{0,6},{2,4},{4,2},{6,0},{8,14},{10,12},{12,10},{14,8},{1,7},{3,5},... | collective-permute-start | bytes 184328 | tf_op jit(solution)/shard_map/ppermute | solution.py:209

commit v4 on v3

--- a/solution.py
+++ b/solution.py
@@ -70,7 +70,6 @@
     return lax.all_to_all(outputs, "head", split_axis=0, concat_axis=1, tiled=True)
 
 
-CHIP = ("seq", "head")
 BF16 = jnp.bfloat16
 F32 = jnp.float32
 SWAP = [(0, 1), (1, 0)]
@@ -93,20 +92,16 @@
         copy.wait()
     rows, width = q_ref.shape
     part = width // groups
-    full_refs, far_refs = outs[:groups], outs[groups:]
+    pair_refs, query_refs = outs[:groups], outs[groups:]
     q_inverse, k_inverse = inverse_rms(q_ref), inverse_rms(k_ref)
     for step in range(groups):
         group = lax.bitwise_xor(me_ref[0], step)
         columns = pl.ds(pl.multiple_of(group * part, HD), part)
-        v_part = v_ref[:, columns]
-        k_part = (k_ref[:, columns].astype(F32) * k_inverse * kg_ref[:, columns]).astype(BF16)
-        q_part = (q_ref[:, columns].astype(F32) * q_inverse * qg_ref[:, columns]).astype(BF16)
-        full, far = full_refs[step], far_refs[step]
-        far[0:rows, :] = v_part
-        far[rows : 2 * rows, :] = k_part
-        full[0:rows, :] = v_part
-        full[rows : 2 * rows, :] = k_part
-        full[2 * rows : 3 * rows, :] = q_part
+        k_part = k_ref[:, columns].astype(F32) * k_inverse * kg_ref[:, columns]
+        q_part = q_ref[:, columns].astype(F32) * q_inverse * qg_ref[:, columns]
+        pair_refs[step][0:rows, :] = v_ref[:, columns]
+        pair_refs[step][rows : 2 * rows, :] = k_part.astype(BF16)
+        query_refs[step][...] = q_part.astype(BF16)
 
 
 def joined(refs, first, rows, columns):
@@ -114,56 +109,31 @@
     return jnp.concatenate(pieces, axis=0).astype(BF16)
 
 
-def head_scores(q_head, k_head):
+def columns_of(head):
+    return slice(head * HD, (head + 1) * HD)
+
+
+def attend_kernel(groups, *refs):
+    queries, pairs, outs = refs[:groups], refs[groups:-groups], refs[-groups:]
+    rows, width = queries[0].shape
     factor = 1.0 / math.sqrt(HD)
     dims = (((1,), (1,)), ((), ()))
-    return lax.dot_general(q_head, k_head, dims, preferred_element_type=F32) * factor
-
-
-def columns_of(head):
-    return slice(head * HD, (head + 1) * HD)
-
-
-def all_scores(query_refs, key_refs):
-    rows, heads = query_refs[0].shape[0] // 3, query_refs[0].shape[1] // HD
-    scores = []
-    for head in range(heads):
-        q_head = joined(query_refs, 2 * rows, rows, columns_of(head))
-        scores.append(head_scores(q_head, joined(key_refs, rows, rows, columns_of(head))))
-    return scores
-
-
-def near_kernel(groups, *refs):
-    near, (high_ref, sum_ref, acc_ref) = refs[:-3], refs[-3:]
-    rows = near[0].shape[0] // 3
-    all_weights = []
-    for head, scores in enumerate(all_scores(near[:groups], near)):
+    heads = range(width // HD)
+    all_scores = []
+    for head in heads:
+        q_head = joined(queries, 0, rows, columns_of(head))
+        k_head = joined(pairs, rows, rows, columns_of(head))
+        scores = lax.dot_general(q_head, k_head, dims, preferred_element_type=F32)
+        all_scores.append(scores * factor)
+    kept = []
+    for scores in all_scores:
         highest = jnp.max(scores, axis=-1, keepdims=True)
         weights = jnp.exp(scores - highest)
-        high_ref[head] = jnp.broadcast_to(highest, high_ref.shape[1:])
-        weight_sum = jnp.sum(weights, axis=-1, keepdims=True)
-        sum_ref[head] = jnp.broadcast_to(weight_sum, sum_ref.shape[1:])
-        all_weights.append(weights.astype(BF16))
-    for head, weights in enumerate(all_weights):
-        v_head = joined(near, 0, rows, columns_of(head))
-        acc_ref[head] = jnp.dot(weights, v_head, preferred_element_type=F32)
-
-
-def far_kernel(groups, high_ref, sum_ref, acc_ref, *refs):
-    near, far, outs = refs[:groups], refs[groups : 3 * groups], refs[3 * groups :]
-    rows = near[0].shape[0] // 3
-    kept = []
-    for head, scores in enumerate(all_scores(near, far)):
-        before = high_ref[head]
-        highest = jnp.maximum(before, jnp.max(scores, axis=-1, keepdims=True))
-        weights = jnp.exp(scores - highest[:, 0:1])
-        shrink = jnp.exp(before - highest)
-        weight_sum = sum_ref[head] * shrink + jnp.sum(weights, axis=-1, keepdims=True)
-        kept.append((weights.astype(BF16), acc_ref[head] * shrink, weight_sum))
-    for head, (weights, acc, weight_sum) in enumerate(kept):
-        v_head = joined(far, 0, rows, columns_of(head))
-        added = jnp.dot(weights, v_head, preferred_element_type=F32)
-        result = ((acc + added) / weight_sum).astype(BF16)
+        kept.append((weights.astype(BF16), jnp.sum(weights, axis=-1, keepdims=True)))
+    for head, (weights, weight_sum) in zip(heads, kept):
+        v_head = joined(pairs, 0, rows, columns_of(head))
+        weighted = jnp.dot(weights, v_head, preferred_element_type=F32)
+        result = (weighted / weight_sum).astype(BF16)
         for step in range(groups):
             outs[step][:, columns_of(head)] = result[step * rows : (step + 1) * rows, :]
 
@@ -195,25 +165,20 @@
     return call
 
 
-def halves_body(sizes, queries, keys, values, q_gain, k_gain):
-    seq, across = sizes["seq"], sizes["head"]
-    groups = seq // 2 * across
+def columns_body(groups, queries, keys, values, q_gain, k_gain):
     rows, width = queries.shape
     part = width // groups
-    heads = part // HD
-    me = lax.axis_index("seq") % (seq // 2) * across + lax.axis_index("head")
-    me = me.astype(jnp.int32).reshape(1)
-
-    def send(value, half, step):
-        place = half * (seq // 2) * across + step
-        return lax.ppermute(value, CHIP, [(i, i ^ place) for i in range(seq * across)])
-
-    def swap(value):
-        return lax.ppermute(value, "sub", SWAP)
-
+    me = lax.axis_index("seq").astype(jnp.int32).reshape(1)
     steps = range(groups)
-    full = jax.ShapeDtypeStruct((3 * rows, part), BF16)
-    far = jax.ShapeDtypeStruct((2 * rows, part), BF16)
+
+    def send(value, step):
+        return lax.ppermute(value, "seq", [(i, i ^ step) for i in steps])
+
+    def swap(axis, value):
+        return lax.ppermute(value, axis, SWAP)
+
+    pair = jax.ShapeDtypeStruct((2 * rows, part), BF16)
+    piece = jax.ShapeDtypeStruct((rows, part), BF16)
     token = pltpu.VMEM((rows, width), BF16)
     gain = pltpu.VMEM((1, width), F32)
     held = [
@@ -222,25 +187,22 @@
     ]
     packed = kernel_call(
         functools.partial(pack_kernel, groups),
-        [full] * groups + [far] * groups,
+        [pair] * groups + [piece] * groups,
         scalars=1,
         fetched=range(1, 6),
         scratch=[token] * 3 + [gain] * 2 + [pltpu.SemaphoreType.DMA((5,))],
     )(me, *held)
-    fulls, fars = packed[:groups], packed[groups:]
-    far_in = [send(fars[step], 1, step) for step in steps]
-    near_in = [fulls[0]] + [send(fulls[step], 0, step) for step in steps[1:]]
-    near_other = [swap(near_in[step]) for step in steps]
-    far_other = [swap(far_in[step]) for step in steps]
-    state = jax.ShapeDtypeStruct((heads, groups * rows, HD), F32)
-    partial = kernel_call(functools.partial(near_kernel, groups), [state] * 3)(
-        *near_in, *near_other
-    )
-    piece = jax.ShapeDtypeStruct((rows, part), BF16)
-    pieces = kernel_call(functools.partial(far_kernel, groups), [piece] * groups)(
-        *partial, *near_in, *far_in, *far_other
-    )
-    back = [pieces[0]] + [send(pieces[step], 0, step) for step in steps[1:]]
+    pairs, asked = packed[:groups], packed[groups:]
+    mine = [pairs[0]] + [send(pairs[step], step) for step in steps[1:]]
+    asked = [asked[0]] + [send(asked[step], step) for step in steps[1:]]
+    beside = [swap("head", mine[step]) for step in steps]
+    blocks = mine + beside
+    blocks += [swap("sub", mine[step]) for step in steps]
+    blocks += [swap("sub", beside[step]) for step in steps]
+    pieces = kernel_call(functools.partial(attend_kernel, groups), [piece] * groups)(
+        *asked, *blocks
+    )
+    back = [pieces[0]] + [send(pieces[step], step) for step in steps[1:]]
     whole = jax.ShapeDtypeStruct((rows, width), BF16)
     return kernel_call(functools.partial(place_kernel, groups), whole, scalars=1)(me, *back)
 
@@ -251,13 +213,12 @@
 
 def solution(mesh):
     sizes = mesh.shape
-    groups = sizes["seq"] // 2 * sizes["head"]
-    paired = sizes["sub"] == 2 and sizes["seq"] > 1
-    paired = paired and power_of_two(sizes["seq"]) and power_of_two(sizes["head"])
+    groups = sizes["seq"]
+    paired = sizes["sub"] == 2 and sizes["head"] == 2 and power_of_two(groups)
 
     def body(queries, *rest):
         if paired and queries.shape[1] // HD % groups == 0:
-            return halves_body(sizes, queries, *rest)
+            return columns_body(groups, queries, *rest)
         return gathered_body(queries, *rest)
 
     token_spec = P(("grp", "seq", "head", "sub"), None)

time: 42.3 us -> 44.4 us (1.050)
  starting transfers between devices: 18.6 us -> 20.2 us
  waiting for transfers between devices: 19.5 us -> 20.8 us
  Pallas kernels: 3.99 us -> 3.11 us
    ppermute x18 -> x21, starting transfers between devices: 18.6 us -> 20.2 us  [the longest x9 14.5 us: send(): return lax.ppermute(value, 'seq', [(i, i ^ step) for i in steps])]
    ppermute x18 -> x21, waiting for transfers between devices: 19.5 us -> 20.8 us  [the longest x9 13.5 us: send(): return lax.ppermute(value, 'seq', [(i, i ^ step) for i in steps])]
    pallas_call x4 -> x3, Pallas kernels: 3.99 us -> 3.11 us  [call(): pl.pallas_call(kernel, out_shape=shapes, in_specs=places, out_specs=jax.t...]
  transfers between devices with their start and end apart: 18 -> 21, of which waited for: 7 -> 8; matrix products, arithmetic and copies ran while one was open for 0% -> 0% of each run, Pallas kernels for 2% -> 0%
where the time goes in v4:
time: 44.4 us; the launch traced here: 44.2 us
  waiting for transfers between devices  20.8 us (47%)
  starting transfers between devices  20.2 us (45%)
  Pallas kernels  3.11 us (7%)
    ppermute x9, starting transfers between devices, send(): return lax.ppermute(value, 'seq', [(i, i ^ step) for i in steps])  14.5 us
    ppermute x9, waiting for transfers between devices, send(): return lax.ppermute(value, 'seq', [(i, i ^ step) for i in steps])  13.5 us
    ppermute x12, waiting for transfers between devices, swap(): return lax.ppermute(value, axis, SWAP)  7.35 us
    ppermute x12, starting transfers between devices, swap(): return lax.ppermute(value, axis, SWAP)  5.67 us
    pallas_call x3, Pallas kernels, call(): pl.pallas_call(kernel, out_shape=shapes, in_specs=places, out_specs=jax.t...  3.11 us
  transfers between devices with their start and end apart: 21, of which 8 were waited for; matrix products, arithmetic and copies ran while one was open for 0% of the time, Pallas kernels for 0%

profile of v4, /device:TPU:0, one launch (start us, length us, event | category | flops | bytes accessed | tf_op | source)
XLA Modules:
  0.0 44.2 jit_solution(258664143948027333)
XLA Ops:
  0.0 1.5 %shard_map.55 = (bf16[48,1280]{1,0:T(8,128)(2,1)S(1)}, bf16[48,1280]{1,0:T(8,128)(2,1)S(1)}, bf16[48,1280]{1,0:T(8,128)(2,1)S(1)}, bf16[48,1280]{1,0:T(8,128)(2,...) custom-call(s32[1]{0:T(128)} %bitcast.me_ref, ...), custom_call_target="tpu_custom_call" | custom-call | tf_op jit(solution)/shard_map/pallas_call | solution.py:156
  1.5 3.1 %collective-permute-start = (bf16[24,1280]{1,0:T(8,128)(2,1)S(1)}, bf16[24,1280]{1,0:T(8,128)(2,1)S(1)}, u32[]{:S(2)}, u32[]{:S(2)}) collective-permute-start(bf16[24,1280]{1,0:T(8,128)(2,1)S(1)} %get-tuple-element.18), channel_id=1, source_target_pairs={{0,4},{4,0},{8,12},{12,8},{1,5},{5,1},{9,13},{13,9},{2,6},{6,2},{1... | collective-permute-start | bytes 184328 | tf_op jit(solution)/shard_map/ppermute | solution.py:175
  4.6 2.6 %collective-permute-start.1 = (bf16[24,1280]{1,0:T(8,128)(2,1)S(1)}, bf16[24,1280]{1,0:T(8,128)(2,1)S(1)}, u32[]{:S(2)}, u32[]{:S(2)}) collective-permute-start(bf16[24,1280]{1,0:T(8,128)(2,1)S(1)} %get-tuple-element.19), channel_id=1, source_target_pairs={{0,8},{4,12},{8,0},{12,4},{1,9},{5,13},{9,1},{13,5},{2,10},{6,14},... | collective-permute-start | bytes 184328 | tf_op jit(solution)/shard_map/ppermute | solution.py:175
  7.2 0.0 collective-permute-start.2
  7.2 0.9 %collective-permute-start.3 = (bf16[48,1280]{1,0:T(8,128)(2,1)S(1)}, bf16[48,1280]{1,0:T(8,128)(2,1)S(1)}, u32[]{:S(2)}, u32[]{:S(2)}) collective-permute-start(bf16[48,1280]{1,0:T(8,128)(2,1)S(1)} %get-tuple-element.22), channel_id=1, source_target_pairs={{0,4},{4,0},{8,12},{12,8},{1,5},{5,1},{9,13},{13,9},{2,6},{6,2},{1... | collective-permute-start | bytes 368648 | tf_op jit(solution)/shard_map/ppermute | solution.py:175
  8.1 3.5 %collective-permute-start.4 = (bf16[48,1280]{1,0:T(8,128)(2,1)S(1)}, bf16[48,1280]{1,0:T(8,128)(2,1)S(1)}, u32[]{:S(2)}, u32[]{:S(2)}) collective-permute-start(bf16[48,1280]{1,0:T(8,128)(2,1)S(1)} %get-tuple-element.23), channel_id=1, source_target_pairs={{0,8},{4,12},{8,0},{12,4},{1,9},{5,13},{9,1},{13,5},{2,10},{6,14},... | collective-permute-start | bytes 368648 | tf_op jit(solution)/shard_map/ppermute | solution.py:175
  11.6 0.0 collective-permute-done.refs_1_
  11.6 0.0 collective-permute-start.5
  11.6 0.0 collective-permute-done.1.refs_2_
  11.6 0.1 collective-permute-start.10
  11.7 2.3 %collective-permute-done.2.refs_3_ = bf16[24,1280]{1,0:T(8,128)(2,1)S(1)} collective-permute-done((bf16[24,1280]{1,0:T(8,128)(2,1)S(1)}, bf16[24,1280]{1,0:T(8,128)(2,1)S(1)}, u32[]{:S(2)}, u32[]{:S(2)}) %collective-permute-start.2) | collective-permute-done | bytes 61472 | tf_op jit(solution)/shard_map/ppermute | solution.py:175
  14.0 1.5 %collective-permute-start.6 = (bf16[48,1280]{1,0:T(8,128)(2,1)S(1)}, bf16[48,1280]{1,0:T(8,128)(2,1)S(1)}, u32[]{:S(2)}, u32[]{:S(2)}) collective-permute-start(bf16[48,1280]{1,0:T(8,128)(2,1)S(1)} %get-tuple-element.21.refs_4_), channel_id=1, source_target_pairs={{0,2},{2,0},{1,3},{3,1},{4,6},{6,4},{5,7},{7,5},{8,10},{10,8},{9,1... | collective-permute-start | bytes 368648 | tf_op jit(solution)/shard_map/ppermute | solution.py:178
  15.5 0.0 collective-permute-done.3.refs_5_
  15.5 0.0 collective-permute-start.11
  15.5 6.0 %collective-permute-done.4.refs_6_ = bf16[48,1280]{1,0:T(8,128)(2,1)S(1)} collective-permute-done((bf16[48,1280]{1,0:T(8,128)(2,1)S(1)}, bf16[48,1280]{1,0:T(8,128)(2,1)S(1)}, u32[]{:S(2)}, u32[]{:S(2)}) %collective-permute-start.4) | collective-permute-done | bytes 122912 | tf_op jit(solution)/shard_map/ppermute | solution.py:175
  21.5 1.5 %collective-permute-start.7 = (bf16[48,1280]{1,0:T(8,128)(2,1)S(1)}, bf16[48,1280]{1,0:T(8,128)(2,1)S(1)}, u32[]{:S(2)}, u32[]{:S(2)}) collective-permute-start(bf16[48,1280]{1,0:T(8,128)(2,1)S(1)} %collective-permute-done.3.refs_5_), channel_id=1, source_target_pairs={{0,2},{2,0},{1,3},{3,1},{4,6},{6,4},{5,7},{7,5},{8,10},{10,8},{9,1... | collective-permute-start | bytes 368648 | tf_op jit(solution)/shard_map/ppermute | solution.py:178
  23.0 0.0 collective-permute-done.5.refs_7_
  23.0 0.0 collective-permute-start.12
  23.0 0.0 collective-permute-done.10.refs_12_
  23.0 0.6 %collective-permute-start.8 = (bf16[48,1280]{1,0:T(8,128)(2,1)S(1)}, bf16[48,1280]{1,0:T(8,128)(2,1)S(1)}, u32[]{:S(2)}, u32[]{:S(2)}) collective-permute-start(bf16[48,1280]{1,0:T(8,128)(2,1)S(1)} %collective-permute-done.4.refs_6_), channel_id=1, source_target_pairs={{0,2},{2,0},{1,3},{3,1},{4,6},{6,4},{5,7},{7,5},{8,10},{10,8},{9,1... | collective-permute-start | bytes 368648 | tf_op jit(solution)/shard_map/ppermute | solution.py:178
  23.6 0.0 collective-permute-done.6.refs_8_
  23.6 1.5 %collective-permute-start.9 = (bf16[48,1280]{1,0:T(8,128)(2,1)S(1)}, bf16[48,1280]{1,0:T(8,128)(2,1)S(1)}, u32[]{:S(2)}, u32[]{:S(2)}) collective-permute-start(bf16[48,1280]{1,0:T(8,128)(2,1)S(1)} %collective-permute-done.5.refs_7_), channel_id=1, source_target_pairs={{0,2},{2,0},{1,3},{3,1},{4,6},{6,4},{5,7},{7,5},{8,10},{10,8},{9,1... | collective-permute-start | bytes 368648 | tf_op jit(solution)/shard_map/ppermute | solution.py:178
  25.1 0.0 collective-permute-done.11.refs_13_
  25.1 0.0 collective-permute-start.13
  25.1 1.5 %collective-permute-done.7.refs_9_ = bf16[48,1280]{1,0:T(8,128)(2,1)S(1)} collective-permute-done((bf16[48,1280]{1,0:T(8,128)(2,1)S(1)}, bf16[48,1280]{1,0:T(8,128)(2,1)S(1)}, u32[]{:S(2)}, u32[]{:S(2)}) %collective-permute-start.7) | collective-permute-done | bytes 122912 | tf_op jit(solution)/shard_map/ppermute | solution.py:178
  26.6 0.0 collective-permute-start.14
  26.6 0.0 collective-permute-done.12.refs_14_
  26.6 0.5 %collective-permute-start.15 = (bf16[48,1280]{1,0:T(8,128)(2,1)S(1)}, bf16[48,1280]{1,0:T(8,128)(2,1)S(1)}, u32[]{:S(2)}, u32[]{:S(2)}) collective-permute-start(bf16[48,1280]{1,0:T(8,128)(2,1)S(1)} %collective-permute-done.7.refs_9_), channel_id=1, source_target_pairs={{0,1},{1,0},{2,3},{3,2},{4,5},{5,4},{6,7},{7,6},{8,9},{9,8},{10,11... | collective-permute-start | bytes 368648 | tf_op jit(solution)/shard_map/ppermute | solution.py:178
  27.1 2.1 %collective-permute-done.8.refs_10_ = bf16[48,1280]{1,0:T(8,128)(2,1)S(1)} collective-permute-done((bf16[48,1280]{1,0:T(8,128)(2,1)S(1)}, bf16[48,1280]{1,0:T(8,128)(2,1)S(1)}, u32[]{:S(2)}, u32[]{:S(2)}) %collective-permute-start.8) | collective-permute-done | bytes 122912 | tf_op jit(solution)/shard_map/ppermute | solution.py:178
  29.3 0.0 collective-permute-start.16
  29.3 2.4 %collective-permute-done.9.refs_11_ = bf16[48,1280]{1,0:T(8,128)(2,1)S(1)} collective-permute-done((bf16[48,1280]{1,0:T(8,128)(2,1)S(1)}, bf16[48,1280]{1,0:T(8,128)(2,1)S(1)}, u32[]{:S(2)}, u32[]{:S(2)}) %collective-permute-start.9) | collective-permute-done | bytes 122912 | tf_op jit(solution)/shard_map/ppermute | solution.py:178
  31.6 0.0 collective-permute-start.17
  31.6 0.0 collective-permute-done.13.refs_15_
  31.6 0.0 collective-permute-done.14.refs_16_
  31.6 0.0 collective-permute-done.15.refs_17_
  31.6 0.0 collective-permute-done.16.refs_18_
  31.7 1.3 %collective-permute-done.17.refs_19_ = bf16[48,1280]{1,0:T(8,128)(2,1)S(1)} collective-permute-done((bf16[48,1280]{1,0:T(8,128)(2,1)S(1)}, bf16[48,1280]{1,0:T(8,128)(2,1)S(1)}, u32[]{:S(2)}, u32[]{:S(2)}) %collective-permute-start.17) | collective-permute-done | bytes 122912 | tf_op jit(solution)/shard_map/ppermute | solution.py:178
  33.0 0.9 %shard_map.56 = (bf16[24,1280]{1,0:T(8,128)(2,1)S(1)}, bf16[24,1280]{1,0:T(8,128)(2,1)S(1)}, bf16[24,1280]{1,0:T(8,128)(2,1)S(1)}, bf16[24,1280]{1,0:T(8,128)(2,1)S(1)}) custom-call(bf16[24,1280]{1,0:T(8,128)(2,1)S(1)} %get-tuple-element.17.refs_0_, bf16[24,1280]{1,0:T(8,128)(2,1)S(1)} %collective-permute-done.refs_1_, ...), custom_call_target="tpu_custom_call" | custom-call | tf_op jit(solution)/shard_map/pallas_call | solution.py:156
  33.9 0.8 %collective-permute-start.18 = (bf16[24,1280]{1,0:T(8,128)(2,1)S(1)}, bf16[24,1280]{1,0:T(8,128)(2,1)S(1)}, u32[]{:S(2)}, u32[]{:S(2)}) collective-permute-start(bf16[24,1280]{1,0:T(8,128)(2,1)S(1)} %get-tuple-element.26), channel_id=1, source_target_pairs={{0,4},{4,0},{8,12},{12,8},{1,5},{5,1},{9,13},{13,9},{2,6},{6,2},{1... | collective-permute-start | bytes 184328 | tf_op jit(solution)/shard_map/ppermute | solution.py:175
  34.7 2.7 %collective-permute-start.19 = (bf16[24,1280]{1,0:T(8,128)(2,1)S(1)}, bf16[24,1280]{1,0:T(8,128)(2,1)S(1)}, u32[]{:S(2)}, u32[]{:S(2)}) collective-permute-start(bf16[24,1280]{1,0:T(8,128)(2,1)S(1)} %get-tuple-element.27), channel_id=1, source_target_pairs={{0,8},{4,12},{8,0},{12,4},{1,9},{5,13},{9,1},{13,5},{2,10},{6,14},... | collective-permute-start | bytes 184328 | tf_op jit(solution)/shard_map/ppermute | solution.py:175
  37.4 0.9 %collective-permute-start.20 = (bf16[24,1280]{1,0:T(8,128)(2,1)S(1)}, bf16[24,1280]{1,0:T(8,128)(2,1)S(1)}, u32[]{:S(2)}, u32[]{:S(2)}) collective-permute-start(bf16[24,1280]{1,0:T(8,128)(2,1)S(1)} %get-tuple-element.28), channel_id=1, source_target_pairs={{0,12},{4,8},{8,4},{12,0},{1,13},{5,9},{9,5},{13,1},{2,14},{6,10},... | collective-permute-start | bytes 184328 | tf_op jit(solution)/shard_map/ppermute | solution.py:175
  38.3 0.0 collective-permute-done.18.refs_1_
  38.3 3.0 %collective-permute-done.19.refs_2_ = bf16[24,1280]{1,0:T(8,128)(2,1)S(1)} collective-permute-done((bf16[24,1280]{1,0:T(8,128)(2,1)S(1)}, bf16[24,1280]{1,0:T(8,128)(2,1)S(1)}, u32[]{:S(2)}, u32[]{:S(2)}) %collective-permute-start.19) | collective-permute-done | bytes 61472 | tf_op jit(solution)/shard_map/ppermute | solution.py:175
  41.3 2.2 %collective-permute-done.20.refs_3_ = bf16[24,1280]{1,0:T(8,128)(2,1)S(1)} collective-permute-done((bf16[24,1280]{1,0:T(8,128)(2,1)S(1)}, bf16[24,1280]{1,0:T(8,128)(2,1)S(1)}, u32[]{:S(2)}, u32[]{:S(2)}) %collective-permute-start.20) | collective-permute-done | bytes 61472 | tf_op jit(solution)/shard_map/ppermute | solution.py:175
  43.5 0.7 %shard_map.57 = bf16[24,5120]{1,0:T(8,128)(2,1)} custom-call(s32[1]{0:T(128)} %bitcast.me_ref, bf16[24,1280]{1,0:T(8,128)(2,1)S(1)} %get-tuple-element.25.refs_0_, bf16[24,1280]{1,0:T(8,128)(2,1)S(1)} %collective-permute-done.18.refs_1_, bf16[24,1280]{1,0:T(8,128)(2,1)S(1)} %collective-permute-done.19.refs_2_, ...), custom_call_target="tpu_custom_call" | custom-call | tf_op jit(solution)/shard_map/pallas_call | solution.py:156
Async XLA Ops:
  1.5 10.1 %collective-permute-start = (bf16[24,1280]{1,0:T(8,128)(2,1)S(1)}, bf16[24,1280]{1,0:T(8,128)(2,1)S(1)}, u32[]{:S(2)}, u32[]{:S(2)}) collective-permute-start(bf16[24,1280]{1,0:T(8,128)(2,1)S(1)} %get-tuple-element.18), channel_id=1, source_target_pairs={{0,4},{4,0},{8,12},{12,8},{1,5},{5,1},{9,13},{13,9},{2,6},{6,2},{1... | collective-permute-start | bytes 184328 | tf_op jit(solution)/shard_map/ppermute | solution.py:175
  4.6 7.0 %collective-permute-start.1 = (bf16[24,1280]{1,0:T(8,128)(2,1)S(1)}, bf16[24,1280]{1,0:T(8,128)(2,1)S(1)}, u32[]{:S(2)}, u32[]{:S(2)}) collective-permute-start(bf16[24,1280]{1,0:T(8,128)(2,1)S(1)} %get-tuple-element.19), channel_id=1, source_target_pairs={{0,8},{4,12},{8,0},{12,4},{1,9},{5,13},{9,1},{13,5},{2,10},{6,14},... | collective-permute-start | bytes 184328 | tf_op jit(solution)/shard_map/ppermute | solution.py:175
  7.2 6.8 %collective-permute-start.2 = (bf16[24,1280]{1,0:T(8,128)(2,1)S(1)}, bf16[24,1280]{1,0:T(8,128)(2,1)S(1)}, u32[]{:S(2)}, u32[]{:S(2)}) collective-permute-start(bf16[24,1280]{1,0:T(8,128)(2,1)S(1)} %get-tuple-element.20), channel_id=1, source_target_pairs={{0,12},{4,8},{8,4},{12,0},{1,13},{5,9},{9,5},{13,1},{2,14},{6,10},... | collective-permute-start | bytes 184328 | tf_op jit(solution)/shard_map/ppermute | solution.py:175
  7.2 8.3 %collective-permute-start.3 = (bf16[48,1280]{1,0:T(8,128)(2,1)S(1)}, bf16[48,1280]{1,0:T(8,128)(2,1)S(1)}, u32[]{:S(2)}, u32[]{:S(2)}) collective-permute-start(bf16[48,1280]{1,0:T(8,128)(2,1)S(1)} %get-tuple-element.22), channel_id=1, source_target_pairs={{0,4},{4,0},{8,12},{12,8},{1,5},{5,1},{9,13},{13,9},{2,6},{6,2},{1... | collective-permute-start | bytes 368648 | tf_op jit(solution)/shard_map/ppermute | solution.py:175
  8.1 13.4 %collective-permute-start.4 = (bf16[48,1280]{1,0:T(8,128)(2,1)S(1)}, bf16[48,1280]{1,0:T(8,128)(2,1)S(1)}, u32[]{:S(2)}, u32[]{:S(2)}) collective-permute-start(bf16[48,1280]{1,0:T(8,128)(2,1)S(1)} %get-tuple-element.23), channel_id=1, source_target_pairs={{0,8},{4,12},{8,0},{12,4},{1,9},{5,13},{9,1},{13,5},{2,10},{6,14},... | collective-permute-start | bytes 368648 | tf_op jit(solution)/shard_map/ppermute | solution.py:175
  11.6 11.4 %collective-permute-start.5 = (bf16[48,1280]{1,0:T(8,128)(2,1)S(1)}, bf16[48,1280]{1,0:T(8,128)(2,1)S(1)}, u32[]{:S(2)}, u32[]{:S(2)}) collective-permute-start(bf16[48,1280]{1,0:T(8,128)(2,1)S(1)} %get-tuple-element.24), channel_id=1, source_target_pairs={{0,12},{4,8},{8,4},{12,0},{1,13},{5,9},{9,5},{13,1},{2,14},{6,10},... | collective-permute-start | bytes 368648 | tf_op jit(solution)/shard_map/ppermute | solution.py:175
  11.6 11.4 %collective-permute-start.10 = (bf16[48,1280]{1,0:T(8,128)(2,1)S(1)}, bf16[48,1280]{1,0:T(8,128)(2,1)S(1)}, u32[]{:S(2)}, u32[]{:S(2)}) collective-permute-start(bf16[48,1280]{1,0:T(8,128)(2,1)S(1)} %get-tuple-element.21.refs_4_), channel_id=1, source_target_pairs={{0,1},{1,0},{2,3},{3,2},{4,5},{5,4},{6,7},{7,6},{8,9},{9,8},{10,11... | collective-permute-start | bytes 368648 | tf_op jit(solution)/shard_map/ppermute | solution.py:178
  14.0 9.6 %collective-permute-start.6 = (bf16[48,1280]{1,0:T(8,128)(2,1)S(1)}, bf16[48,1280]{1,0:T(8,128)(2,1)S(1)}, u32[]{:S(2)}, u32[]{:S(2)}) collective-permute-start(bf16[48,1280]{1,0:T(8,128)(2,1)S(1)} %get-tuple-element.21.refs_4_), channel_id=1, source_target_pairs={{0,2},{2,0},{1,3},{3,1},{4,6},{6,4},{5,7},{7,5},{8,10},{10,8},{9,1... | collective-permute-start | bytes 368648 | tf_op jit(solution)/shard_map/ppermute | solution.py:178
  15.5 9.6 %collective-permute-start.11 = (bf16[48,1280]{1,0:T(8,128)(2,1)S(1)}, bf16[48,1280]{1,0:T(8,128)(2,1)S(1)}, u32[]{:S(2)}, u32[]{:S(2)}) collective-permute-start(bf16[48,1280]{1,0:T(8,128)(2,1)S(1)} %collective-permute-done.3.refs_5_), channel_id=1, source_target_pairs={{0,1},{1,0},{2,3},{3,2},{4,5},{5,4},{6,7},{7,6},{8,9},{9,8},{10,11... | collective-permute-start | bytes 368648 | tf_op jit(solution)/shard_map/ppermute | solution.py:178
  21.5 5.2 %collective-permute-start.7 = (bf16[48,1280]{1,0:T(8,128)(2,1)S(1)}, bf16[48,1280]{1,0:T(8,128)(2,1)S(1)}, u32[]{:S(2)}, u32[]{:S(2)}) collective-permute-start(bf16[48,1280]{1,0:T(8,128)(2,1)S(1)} %collective-permute-done.3.refs_5_), channel_id=1, source_target_pairs={{0,2},{2,0},{1,3},{3,1},{4,6},{6,4},{5,7},{7,5},{8,10},{10,8},{9,1... | collective-permute-start | bytes 368648 | tf_op jit(solution)/shard_map/ppermute | solution.py:178
  23.0 3.7 %collective-permute-start.12 = (bf16[48,1280]{1,0:T(8,128)(2,1)S(1)}, bf16[48,1280]{1,0:T(8,128)(2,1)S(1)}, u32[]{:S(2)}, u32[]{:S(2)}) collective-permute-start(bf16[48,1280]{1,0:T(8,128)(2,1)S(1)} %collective-permute-done.4.refs_6_), channel_id=1, source_target_pairs={{0,1},{1,0},{2,3},{3,2},{4,5},{5,4},{6,7},{7,6},{8,9},{9,8},{10,11... | collective-permute-start | bytes 368648 | tf_op jit(solution)/shard_map/ppermute | solution.py:178
  23.0 6.3 %collective-permute-start.8 = (bf16[48,1280]{1,0:T(8,128)(2,1)S(1)}, bf16[48,1280]{1,0:T(8,128)(2,1)S(1)}, u32[]{:S(2)}, u32[]{:S(2)}) collective-permute-start(bf16[48,1280]{1,0:T(8,128)(2,1)S(1)} %collective-permute-done.4.refs_6_), channel_id=1, source_target_pairs={{0,2},{2,0},{1,3},{3,1},{4,6},{6,4},{5,7},{7,5},{8,10},{10,8},{9,1... | collective-permute-start | bytes 368648 | tf_op jit(solution)/shard_map/ppermute | solution.py:178
  23.6 8.0 %collective-permute-start.9 = (bf16[48,1280]{1,0:T(8,128)(2,1)S(1)}, bf16[48,1280]{1,0:T(8,128)(2,1)S(1)}, u32[]{:S(2)}, u32[]{:S(2)}) collective-permute-start(bf16[48,1280]{1,0:T(8,128)(2,1)S(1)} %collective-permute-done.5.refs_7_), channel_id=1, source_target_pairs={{0,2},{2,0},{1,3},{3,1},{4,6},{6,4},{5,7},{7,5},{8,10},{10,8},{9,1... | collective-permute-start | bytes 368648 | tf_op jit(solution)/shard_map/ppermute | solution.py:178
  25.1 6.6 %collective-permute-start.13 = (bf16[48,1280]{1,0:T(8,128)(2,1)S(1)}, bf16[48,1280]{1,0:T(8,128)(2,1)S(1)}, u32[]{:S(2)}, u32[]{:S(2)}) collective-permute-start(bf16[48,1280]{1,0:T(8,128)(2,1)S(1)} %collective-permute-done.5.refs_7_), channel_id=1, source_target_pairs={{0,1},{1,0},{2,3},{3,2},{4,5},{5,4},{6,7},{7,6},{8,9},{9,8},{10,11... | collective-permute-start | bytes 368648 | tf_op jit(solution)/shard_map/ppermute | solution.py:178
  26.6 5.0 %collective-permute-start.14 = (bf16[48,1280]{1,0:T(8,128)(2,1)S(1)}, bf16[48,1280]{1,0:T(8,128)(2,1)S(1)}, u32[]{:S(2)}, u32[]{:S(2)}) collective-permute-start(bf16[48,1280]{1,0:T(8,128)(2,1)S(1)} %collective-permute-done.6.refs_8_), channel_id=1, source_target_pairs={{0,1},{1,0},{2,3},{3,2},{4,5},{5,4},{6,7},{7,6},{8,9},{9,8},{10,11... | collective-permute-start | bytes 368648 | tf_op jit(solution)/shard_map/ppermute | solution.py:178
  26.6 5.0 %collective-permute-start.15 = (bf16[48,1280]{1,0:T(8,128)(2,1)S(1)}, bf16[48,1280]{1,0:T(8,128)(2,1)S(1)}, u32[]{:S(2)}, u32[]{:S(2)}) collective-permute-start(bf16[48,1280]{1,0:T(8,128)(2,1)S(1)} %collective-permute-done.7.refs_9_), channel_id=1, source_target_pairs={{0,1},{1,0},{2,3},{3,2},{4,5},{5,4},{6,7},{7,6},{8,9},{9,8},{10,11... | collective-permute-start | bytes 368648 | tf_op jit(solution)/shard_map/ppermute | solution.py:178
  29.3 2.4 %collective-permute-start.16 = (bf16[48,1280]{1,0:T(8,128)(2,1)S(1)}, bf16[48,1280]{1,0:T(8,128)(2,1)S(1)}, u32[]{:S(2)}, u32[]{:S(2)}) collective-permute-start(bf16[48,1280]{1,0:T(8,128)(2,1)S(1)} %collective-permute-done.8.refs_10_), channel_id=1, source_target_pairs={{0,1},{1,0},{2,3},{3,2},{4,5},{5,4},{6,7},{7,6},{8,9},{9,8},{10,11... | collective-permute-start | bytes 368648 | tf_op jit(solution)/shard_map/ppermute | solution.py:178
  31.6 1.3 %collective-permute-start.17 = (bf16[48,1280]{1,0:T(8,128)(2,1)S(1)}, bf16[48,1280]{1,0:T(8,128)(2,1)S(1)}, u32[]{:S(2)}, u32[]{:S(2)}) collective-permute-start(bf16[48,1280]{1,0:T(8,128)(2,1)S(1)} %collective-permute-done.9.refs_11_), channel_id=1, source_target_pairs={{0,1},{1,0},{2,3},{3,2},{4,5},{5,4},{6,7},{7,6},{8,9},{9,8},{10,11... | collective-permute-start | bytes 368648 | tf_op jit(solution)/shard_map/ppermute | solution.py:178
  33.9 4.5 %collective-permute-start.18 = (bf16[24,1280]{1,0:T(8,128)(2,1)S(1)}, bf16[24,1280]{1,0:T(8,128)(2,1)S(1)}, u32[]{:S(2)}, u32[]{:S(2)}) collective-permute-start(bf16[24,1280]{1,0:T(8,128)(2,1)S(1)} %get-tuple-element.26), channel_id=1, source_target_pairs={{0,4},{4,0},{8,12},{12,8},{1,5},{5,1},{9,13},{13,9},{2,6},{6,2},{1... | collective-permute-start | bytes 184328 | tf_op jit(solution)/shard_map/ppermute | solution.py:175
  34.7 6.6 %collective-permute-start.19 = (bf16[24,1280]{1,0:T(8,128)(2,1)S(1)}, bf16[24,1280]{1,0:T(8,128)(2,1)S(1)}, u32[]{:S(2)}, u32[]{:S(2)}) collective-permute-start(bf16[24,1280]{1,0:T(8,128)(2,1)S(1)} %get-tuple-element.27), channel_id=1, source_target_pairs={{0,8},{4,12},{8,0},{12,4},{1,9},{5,13},{9,1},{13,5},{2,10},{6,14},... | collective-permute-start | bytes 184328 | tf_op jit(solution)/shard_map/ppermute | solution.py:175
  37.4 6.1 %collective-permute-start.20 = (bf16[24,1280]{1,0:T(8,128)(2,1)S(1)}, bf16[24,1280]{1,0:T(8,128)(2,1)S(1)}, u32[]{:S(2)}, u32[]{:S(2)}) collective-permute-start(bf16[24,1280]{1,0:T(8,128)(2,1)S(1)} %get-tuple-element.28), channel_id=1, source_target_pairs={{0,12},{4,8},{8,4},{12,0},{1,13},{5,9},{9,5},{13,1},{2,14},{6,10},... | collective-permute-start | bytes 184328 | tf_op jit(solution)/shard_map/ppermute | solution.py:175
